TPU v7x, 32 devices: a whole 2x2x4 slice. The times are simulated.
32 devices in a mesh: enc: 2 (over x), dp: 16 (over z, y, core).
Axes of the slice: x: 2, y: 2, z: 4, core: 2. Of those that a mesh axis runs over, the one named last changes fastest.
Arguments:
- hidden_in: bfloat16 [2, 48, 256, 768], P('enc', 'dp'), may hold values from -6 to 6
- starts: int32 [2, 48, 4], P('enc', 'dp'), may hold values from 0 to 192, as said below
- positives: int32 [192], replicated, may hold values from 0 to 191, each once
- qkv_weight: bfloat16 [2, 768, 2304], P('enc'), may hold values from -0.21875 to 0.21875
- query_bias: float32 [2, 768], P('enc'), may hold values from -3 to 3
- value_bias: float32 [2, 768], P('enc'), may hold values from -3 to 3
- out_weight: bfloat16 [2, 768, 768], P('enc'), may hold values from -0.625 to 0.625
- out_bias: float32 [2, 768], P('enc'), may hold values from -3 to 3
- first_gain: float32 [2, 768], P('enc'), may hold values from 0.5 to 1.5
- first_shift: float32 [2, 768], P('enc'), may hold values from -3 to 3
- up_weight: bfloat16 [2, 768, 3072], P('enc'), may hold values from -0.21875 to 0.21875
- up_bias: float32 [2, 3072], P('enc'), may hold values from -3 to 3
- down_weight: bfloat16 [2, 3072, 768], P('enc'), may hold values from -0.109375 to 0.109375
- down_bias: float32 [2, 768], P('enc'), may hold values from -3 to 3
- second_gain: float32 [2, 768], P('enc'), may hold values from 0.5 to 1.5
- second_shift: float32 [2, 768], P('enc'), may hold values from -3 to 3
Outputs:
- loss_mean: float32 [], replicated
- hidden_out: bfloat16 [2, 48, 256, 768], P('enc', 'dp')
- hidden_grad: bfloat16 [2, 48, 256, 768], P('enc', 'dp')
- grad_qkv: float32 [2, 768, 2304], P('enc')
- grad_query_bias: float32 [2, 768], P('enc')
- grad_value_bias: float32 [2, 768], P('enc')
- grad_out_weight: float32 [2, 768, 768], P('enc')
- grad_out_bias: float32 [2, 768], P('enc')
- grad_first_gain: float32 [2, 768], P('enc')
- grad_first_shift: float32 [2, 768], P('enc')
- grad_up_weight: float32 [2, 768, 3072], P('enc')
- grad_up_bias: float32 [2, 3072], P('enc')
- grad_down_weight: float32 [2, 3072, 768], P('enc')
- grad_down_bias: float32 [2, 768], P('enc')
- grad_second_gain: float32 [2, 768], P('enc')
- grad_second_shift: float32 [2, 768], P('enc')
Inputs may be any that keep to these rules, and one draw needn't show every extreme that they name: starts[e, r] are the first positions of the 4 documents packed into row r of encoder e, rising, the first 0; a document's CLS token stands at its start. For the questions (e = 0) they are 0, 64, 128 and 192; of the passages of a row one is exactly 128 long and the last is 64 long or longer. `positives`: the passage, numbered r * 4 + k over packed rows r and slots k, that answers question q (numbered alike); every passage answers exactly one question.
All inputs are finite; a program needn't handle non-finite values.
Results may differ from a plain program's by a relative error of at most 0.025.
Values may be sent and summed in bfloat16 or wider, within the bound.
A program may use at most 192 MiB of HBM per device.

v0:
```python
import jax
import jax.numpy as jnp
from jax import lax
from jax.sharding import PartitionSpec as P

H = 12
DOCS = 4


EPS_NORM = 1e-12


def partner(value, axis, distance):
    mask = 2**distance
    pairs = [(source, source ^ mask) for source in range(lax.axis_size(axis))]
    return lax.ppermute(value, axis, pairs)


def product(left, right):
    return jnp.dot(left, right, preferred_element_type=jnp.float32)


def layer_stats(hidden):
    centred = hidden - jnp.mean(hidden, -1, keepdims=True)
    inverse = lax.rsqrt(jnp.mean(centred * centred, -1, keepdims=True) + EPS_NORM)
    return (centred * inverse, inverse)


def norm_back(upstream, normal, inverse, gain):
    scaled = upstream * gain
    return inverse * (
        scaled
        - jnp.mean(scaled, -1, keepdims=True)
        - normal * jnp.mean(scaled * normal, -1, keepdims=True)
    )


def on_device(
    hidden_in,
    starts,
    positives,
    qkv_weight,
    query_bias,
    value_bias,
    out_weight,
    out_bias,
    first_gain,
    first_shift,
    up_weight,
    up_bias,
    down_weight,
    down_bias,
    second_gain,
    second_shift,
):
    rows, length, width = (hidden_in.shape[1], hidden_in.shape[2], hidden_in.shape[3])
    heads = H
    head_size = width // heads
    tokens = rows * length
    flat = hidden_in.reshape(tokens, width)
    w_qkv = qkv_weight[0]
    w_out = out_weight[0]
    w_up = up_weight[0]
    w_down = down_weight[0]
    row_starts = starts[0]
    qkv_shift = jnp.concatenate([query_bias[0], jnp.zeros_like(query_bias[0]), value_bias[0]])
    qkv = (product(flat, w_qkv) + qkv_shift).astype(jnp.bfloat16)
    split = qkv.reshape(rows, length, 3, heads, head_size)
    query, key, value = (split[:, :, 0], split[:, :, 1], split[:, :, 2])
    places = jnp.arange(length, dtype=jnp.int32)
    segment = jnp.sum((places[None, :, None] >= row_starts[:, None, :]).astype(jnp.int32), -1)
    allowed = (segment[:, :, None] == segment[:, None, :])[:, None]
    head_scale = head_size ** (-0.5)

    def attention_scores(left, right):
        raw = jnp.einsum("rqhe,rkhe->rhqk", left, right, preferred_element_type=jnp.float32)
        return jnp.where(allowed, head_scale * raw, -1e30)

    scores = attention_scores(query, key)
    peak = jnp.max(scores, -1, keepdims=True)
    log_total = peak + jnp.log(jnp.sum(jnp.exp(scores - peak), -1, keepdims=True))
    weights_low = jnp.exp(scores - log_total).astype(jnp.bfloat16)
    mixed = jnp.einsum("rhqk,rkhe->rqhe", weights_low, value, preferred_element_type=jnp.float32)
    mixed = mixed.astype(jnp.bfloat16).reshape(tokens, width)
    attended = product(mixed, w_out) + out_bias[0]
    first_normal, first_inverse = layer_stats(flat.astype(jnp.float32) + attended)
    normed = first_normal * first_gain[0] + first_shift[0]
    normed_low = normed.astype(jnp.bfloat16)
    inner = product(normed_low, w_up) + up_bias[0]
    activated_low = jax.nn.gelu(inner, approximate=False).astype(jnp.bfloat16)
    outer = product(activated_low, w_down) + down_bias[0]
    second_normal, second_inverse = layer_stats(normed + outer)
    encoded = second_normal * second_gain[0] + second_shift[0]
    hidden_out = encoded.astype(jnp.bfloat16).reshape(1, rows, length, width)
    picker = (places[None, None, :] == row_starts[:, :, None]).astype(jnp.float32)
    cls = jnp.einsum(
        "rdl,rlw->rdw",
        picker,
        encoded.reshape(rows, length, width),
        precision=lax.Precision.HIGHEST,
    )
    local_count = rows * DOCS
    cls_low = cls.reshape(local_count, width).astype(jnp.bfloat16)
    first_half = lax.axis_index("enc") == 0
    mine = lax.all_gather(cls_low, "dp", axis=0, tiled=True)
    other = partner(mine, "enc", 0)
    questions = jnp.where(first_half, mine, other)
    passages = jnp.where(first_half, other, mine)
    count = questions.shape[0]
    sim_scale = width ** (-0.5)
    sims = sim_scale * jnp.einsum(
        "qw,pw->qp", questions, passages, preferred_element_type=jnp.float32
    )
    sim_peak = jnp.max(sims, -1, keepdims=True)
    sim_total = sim_peak + jnp.log(jnp.sum(jnp.exp(sims - sim_peak), -1, keepdims=True))
    target = (jnp.arange(count, dtype=jnp.int32)[None, :] == positives[:, None]).astype(jnp.float32)
    total = jnp.sum(sim_total[:, 0] - jnp.sum(sims * target, -1)) / local_count
    loss_mean = total / lax.axis_size("dp")
    d_sims_low = (sim_scale * (jnp.exp(sims - sim_total) - target) / local_count).astype(
        jnp.bfloat16
    )
    own_start = lax.axis_index("dp") * local_count
    own_rows = lax.dynamic_slice_in_dim(d_sims_low, own_start, local_count, 0)
    own_columns = lax.dynamic_slice_in_dim(d_sims_low, own_start, local_count, 1)
    d_questions = jnp.einsum("qp,pw->qw", own_rows, passages, preferred_element_type=jnp.float32)
    d_passages = jnp.einsum("qp,qw->pw", own_columns, questions, preferred_element_type=jnp.float32)
    d_cls = jnp.where(first_half, d_questions, d_passages).reshape(rows, DOCS, width)
    d_encoded = jnp.einsum("rdl,rdw->rlw", picker, d_cls, precision=lax.Precision.HIGHEST).reshape(
        tokens, width
    )
    grad_second_gain = jnp.sum(d_encoded * second_normal, 0)
    grad_second_shift = jnp.sum(d_encoded, 0)
    d_second = norm_back(d_encoded, second_normal, second_inverse, second_gain[0])
    d_outer_low = d_second.astype(jnp.bfloat16)
    grad_down_bias = jnp.sum(d_outer_low.astype(jnp.float32), 0)
    grad_down_weight = jnp.einsum(
        "tf,tw->fw", activated_low, d_outer_low, preferred_element_type=jnp.float32
    )
    d_activated = jnp.einsum("tw,fw->tf", d_outer_low, w_down, preferred_element_type=jnp.float32)
    normal_cdf = 0.5 * (1.0 + lax.erf(inner * 0.7071067811865476))
    slope = normal_cdf + inner * jnp.exp(-0.5 * inner * inner) * 0.3989422804014327
    d_inner_low = (d_activated * slope).astype(jnp.bfloat16)
    grad_up_bias = jnp.sum(d_inner_low.astype(jnp.float32), 0)
    grad_up_weight = jnp.einsum(
        "tw,tf->wf", normed_low, d_inner_low, preferred_element_type=jnp.float32
    )
    d_normed = d_second + jnp.einsum(
        "tf,wf->tw", d_inner_low, w_up, preferred_element_type=jnp.float32
    )
    grad_first_gain = jnp.sum(d_normed * first_normal, 0)
    grad_first_shift = jnp.sum(d_normed, 0)
    d_first = norm_back(d_normed, first_normal, first_inverse, first_gain[0])
    d_attended_low = d_first.astype(jnp.bfloat16)
    grad_out_bias = jnp.sum(d_attended_low.astype(jnp.float32), 0)
    grad_out_weight = jnp.einsum(
        "tv,tw->vw", mixed, d_attended_low, preferred_element_type=jnp.float32
    )
    d_mixed_low = jnp.einsum(
        "tw,vw->tv", d_attended_low, w_out, preferred_element_type=jnp.float32
    ).astype(jnp.bfloat16)
    d_mixed_heads = d_mixed_low.reshape(rows, length, heads, head_size)
    probs_again = jnp.exp(attention_scores(query, key) - log_total)
    weights_again = probs_again.astype(jnp.bfloat16)
    grad_value = jnp.einsum(
        "rhqk,rqhe->rkhe", weights_again, d_mixed_heads, preferred_element_type=jnp.float32
    )
    d_weights = jnp.einsum(
        "rqhe,rkhe->rhqk", d_mixed_heads, value, preferred_element_type=jnp.float32
    )
    d_scores = probs_again * (d_weights - jnp.sum(d_weights * probs_again, -1, keepdims=True))
    d_raw_low = (head_scale * d_scores).astype(jnp.bfloat16)
    grad_query = jnp.einsum("rhqk,rkhe->rqhe", d_raw_low, key, preferred_element_type=jnp.float32)
    grad_key = jnp.einsum("rhqk,rqhe->rkhe", d_raw_low, query, preferred_element_type=jnp.float32)
    d_qkv_low = (
        jnp.stack([grad_query, grad_key, grad_value], 2)
        .reshape(tokens, 3 * width)
        .astype(jnp.bfloat16)
    )
    grad_qkv_local = jnp.einsum("tw,tv->wv", flat, d_qkv_low, preferred_element_type=jnp.float32)
    bias_sums = jnp.sum(d_qkv_low.astype(jnp.float32), 0)
    grad_query_local = bias_sums[:width]
    grad_value_local = bias_sums[2 * width :]
    d_input = d_first + jnp.einsum(
        "tv,wv->tw", d_qkv_low, w_qkv, preferred_element_type=jnp.float32
    )
    hidden_grad = d_input.astype(jnp.bfloat16).reshape(1, rows, length, width)
    (
        share_qkv,
        share_query_bias,
        share_value_bias,
        share_out_weight,
        share_out_bias,
        share_first_gain,
        share_first_shift,
        share_up_weight,
        share_up_bias,
        share_down_weight,
        share_down_bias,
        share_second_gain,
        share_second_shift,
    ) = (
        lax.psum_scatter(grad_qkv_local[None], "dp", scatter_dimension=1, tiled=True),
        lax.psum_scatter(grad_query_local[None], "dp", scatter_dimension=1, tiled=True),
        lax.psum_scatter(grad_value_local[None], "dp", scatter_dimension=1, tiled=True),
        lax.psum_scatter(grad_out_weight[None], "dp", scatter_dimension=1, tiled=True),
        lax.psum_scatter(grad_out_bias[None], "dp", scatter_dimension=1, tiled=True),
        lax.psum_scatter(grad_first_gain[None], "dp", scatter_dimension=1, tiled=True),
        lax.psum_scatter(grad_first_shift[None], "dp", scatter_dimension=1, tiled=True),
        lax.psum_scatter(grad_up_weight[None], "dp", scatter_dimension=1, tiled=True),
        lax.psum_scatter(grad_up_bias[None], "dp", scatter_dimension=1, tiled=True),
        lax.psum_scatter(grad_down_weight[None], "dp", scatter_dimension=1, tiled=True),
        lax.psum_scatter(grad_down_bias[None], "dp", scatter_dimension=1, tiled=True),
        lax.psum_scatter(grad_second_gain[None], "dp", scatter_dimension=1, tiled=True),
        lax.psum_scatter(grad_second_shift[None], "dp", scatter_dimension=1, tiled=True),
    )
    summed = (
        lax.all_gather(share_qkv.astype(jnp.bfloat16), "dp", axis=1, tiled=True).astype(
            share_qkv.dtype
        ),
        lax.all_gather(share_query_bias.astype(jnp.bfloat16), "dp", axis=1, tiled=True).astype(
            share_query_bias.dtype
        ),
        lax.all_gather(share_value_bias.astype(jnp.bfloat16), "dp", axis=1, tiled=True).astype(
            share_value_bias.dtype
        ),
        lax.all_gather(share_out_weight.astype(jnp.bfloat16), "dp", axis=1, tiled=True).astype(
            share_out_weight.dtype
        ),
        lax.all_gather(share_out_bias.astype(jnp.bfloat16), "dp", axis=1, tiled=True).astype(
            share_out_bias.dtype
        ),
        lax.all_gather(share_first_gain.astype(jnp.bfloat16), "dp", axis=1, tiled=True).astype(
            share_first_gain.dtype
        ),
        lax.all_gather(share_first_shift.astype(jnp.bfloat16), "dp", axis=1, tiled=True).astype(
            share_first_shift.dtype
        ),
        lax.all_gather(share_up_weight.astype(jnp.bfloat16), "dp", axis=1, tiled=True).astype(
            share_up_weight.dtype
        ),
        lax.all_gather(share_up_bias.astype(jnp.bfloat16), "dp", axis=1, tiled=True).astype(
            share_up_bias.dtype
        ),
        lax.all_gather(share_down_weight.astype(jnp.bfloat16), "dp", axis=1, tiled=True).astype(
            share_down_weight.dtype
        ),
        lax.all_gather(share_down_bias.astype(jnp.bfloat16), "dp", axis=1, tiled=True).astype(
            share_down_bias.dtype
        ),
        lax.all_gather(share_second_gain.astype(jnp.bfloat16), "dp", axis=1, tiled=True).astype(
            share_second_gain.dtype
        ),
        lax.all_gather(share_second_shift.astype(jnp.bfloat16), "dp", axis=1, tiled=True).astype(
            share_second_shift.dtype
        ),
    )
    return (
        loss_mean,
        hidden_out,
        hidden_grad,
        summed[0],
        summed[1],
        summed[2],
        summed[3],
        summed[4],
        summed[5],
        summed[6],
        summed[7],
        summed[8],
        summed[9],
        summed[10],
        summed[11],
        summed[12],
    )


def solution(mesh):
    placed = (
        P("enc", "dp", None, None),
        P("enc", "dp", None),
        P(),
        P("enc", None, None),
        P("enc", None),
        P("enc", None),
        P("enc", None, None),
        P("enc", None),
        P("enc", None),
        P("enc", None),
        P("enc", None, None),
        P("enc", None),
        P("enc", None, None),
        P("enc", None),
        P("enc", None),
        P("enc", None),
    )
    return jax.shard_map(
        on_device,
        mesh=mesh,
        in_specs=placed,
        out_specs=(
            P(),
            P("enc", "dp", None, None),
            P("enc", "dp", None, None),
            P("enc", None, None),
            P("enc", None),
            P("enc", None),
            P("enc", None, None),
            P("enc", None),
            P("enc", None),
            P("enc", None),
            P("enc", None, None),
            P("enc", None),
            P("enc", None, None),
            P("enc", None),
            P("enc", None),
            P("enc", None),
        ),
        check_vma=False,
    )
```

profile of v0, /device:TPU:0, one launch (start us, length us, event | category | flops | bytes accessed | tf_op | source)
XLA Modules:
  0.0 1730.8 jit_solution(15230983570294234596)
XLA Ops:
  7.2 1.4 reduce.10
  14.0 5.9 add_convert_fusion
  19.9 11.5 reshape.240
  31.4 7.0 fusion.105
  38.4 4.6 copy.113
  44.5 4.6 copy.115
  49.0 5.1 copy.114
  54.1 3.3 fusion.18
  57.5 2.2 exponential_reduce_fusion
  59.7 1.5 copy-done.1
  61.2 2.3 fusion.55
  66.6 3.4 fusion.108
  70.5 27.3 %fusion.3 = (bf16[768,3072]{1,0:T(8,128)(2,1)S(1)}, f32[768,3072]{1,0:T(8,128)}) fusion(f32[3072]{0:T(1024)S(1)} %bitcast.206, bf16[1,768,3072]{2,1,0:T(8,128)(2,1)} %param.26, f32[768,768]{1,0:T(8,128)S(1)} %get-tuple-element.87, f32[768]{0:T(1024)S(1)} %reduce.7, f32[768]{0:T(1024)S(1)} %reduce.6, f32[768]{0:T(1024)S(1)} %add_rsqrt_fusion.1, ...), kind=kOutput, calls=%fused_computation.5 | convolution fusion | flops 3782541312 | bytes 21258240 | tf_op jit(solution)/shard_map/dot_general | solution.py:20
  97.8 4.1 fusion.109
  102.4 1.5 fusion.104
  103.9 1.5 convolution_convert_fusion.3
  106.7 26.2 %all-gather = bf16[16,12,768]{2,1,0:T(8,128)(2,1)} all-gather(bf16[1,12,768]{2,1,0:T(8,128)(2,1)} %reshape.191), channel_id=1, replica_groups=mesh['enc'=2,'dp'=16] {'dp'}, dimensions={0}, use_global_device_ids=true | all-gather | bytes 313344 | tf_op jit(solution)/shard_map/all_gather | solution.py:105
  132.9 1.8 reshape.192
  134.7 1.5 collective-permute-start
  136.2 8.1 collective-permute-done
  148.8 1.9 convolution_select_fusion
  150.7 1.4 reshape.160
  152.1 3.0 fusion.103
  155.1 2.2 fusion.40
  159.7 3.6 convert_reduce_fusion.2
  163.3 10.9 convert_reduce_fusion
  174.2 5.1 multiply_reduce_fusion.1
  179.3 1.5 convert_reduce_fusion.3
  180.8 1.5 copy-done.9
  182.3 2.5 convolution_bitcast_fusion.3
  185.3 11.0 convolution_bitcast_fusion.2
  196.4 10.8 convolution_bitcast_fusion.1
  207.4 4.1 convolution_convert_fusion.1
  211.6 4.7 reshape.241
  216.2 4.6 copy.78
  220.8 6.8 fusion.70
  227.6 19.2 %fusion.57 = bf16[3,256,1,12,64]{1,4,3,0,2:T(8,128)(2,1)} fusion(f32[3,12,256,256]{2,3,1,0:T(8,128)} %fusion.70, f32[3,12,256]{2,1,0:T(8,128)} %copy-done.18, f32[3,12,256,256]{2,3,1,0:T(8,128)} %copy-done.1, pred[3,256,256]{1,2,0:T(8,128)(4,1)} %broadcast_compare_fusion, bf16[3,256,1,12,64]{1,4,3,0,2:T(8,128)(2,1)} %copy.114), kind=kOutput, calls=%fused_computation.87 | convolution fusion | flops 328541440 | bytes 21467136 | tf_op jit(solution)/shard_map/rhqk,rqhe->rkhe/dot_general | solution.py:173
  246.8 18.1 %fusion.60 = bf16[3,256,1,12,64]{1,4,3,0,2:T(8,128)(2,1)} fusion(f32[3,12,256,256]{2,3,1,0:T(8,128)} %fusion.70, f32[3,12,256]{2,1,0:T(8,128)} %copy-done.18, f32[3,12,256,256]{2,3,1,0:T(8,128)} %copy-done.1, pred[3,256,256]{1,2,0:T(8,128)(4,1)} %broadcast_compare_fusion, bf16[3,256,1,12,64]{1,4,3,0,2:T(8,128)(2,1)} %copy.115), kind=kOutput, calls=%fused_computation.88 | convolution fusion | flops 328541440 | bytes 21467136 | tf_op jit(solution)/shard_map/rhqk,rkhe->rqhe/dot_general | solution.py:172
  264.9 7.5 fusion.56
  272.4 2.1 convert_reduce_fusion.1
  276.9 1.6 reshape_bitcast_fusion.5
  278.6 1.6 reshape_bitcast_fusion.4
  280.3 1.6 reshape_bitcast_fusion.3
  286.2 5.4 copy.83
  291.7 2.8 copy.117
  294.5 1.7 copy.100
  296.2 8.2 convolution_bitcast_fusion
  304.4 16.7 copy.84
  321.1 1.5 convert_element_type.192
  322.8 1226.1 %all-reduce.12 = bf16[1,768,2304]{2,0,1:T(2,128)(2,1)} all-reduce(f32[1,768,2304]{2,0,1:T(1,128)} %copy.84), channel_id=2, replica_groups=mesh['enc'=2,'dp'=16] {'dp'}, use_global_device_ids=true, to_apply=%region_16.17.clone | all-reduce | flops 1769472 | bytes 10616832
  1548.8 1.5 dynamic-slice_convert_fusion
  1551.1 1.8 convert_element_type.201
  1553.0 1.8 convert_element_type.206
  1556.8 6.7 add_convert_fusion.1
  1578.2 1.3 dynamic-update-slice.4
  1580.1 1.3 dynamic-update-slice.6
  1582.1 1.3 dynamic-update-slice.7
  1584.3 1.5 copy.101
  1587.9 67.3 %all-reduce.10 = (bf16[768]{0:T(1024)(128)(2,1)}, bf16[768]{0:T(1024)(128)(2,1)}, bf16[768]{0:T(1024)(128)(2,1)}, bf16[768]{0:T(1024)(128)(2,1)}, bf16[768]{0:T(...) all-reduce(bf16[768]{0:T(1024)(128)(2,1)S(1)} %dynamic-update-slice, ...), channel_id=1, replica_groups=mesh['enc'=2,'dp'=16] {'dp'}, use_global_device_ids=true, to_apply=%add | all-reduce | flops 9216 | bytes 36864
  1666.6 2.8 convert_element_type.193
  1669.4 5.6 convert_element_type.186
  1675.0 7.4 convert_element_type.202
  1682.4 33.5 %all-gather.12.cloned.1.call-done = bf16[1,3072,768]{2,1,0:T(8,128)(2,1)} async-done(((bf16[1,192,768]{2,1,0:T(8,128)(2,1)}), bf16[1,3072,768]{2,1,0:T(8,128)(2,1)}) %all-gather.12.cloned.1.call-update) | async-done | bytes 4718608 | tf_op jit(solution)/shard_map/all_gather | solution.py:244
  1715.9 6.8 convert_element_type.207
  (209 shorter events, 57.2 us)
Async XLA Ops:
  7.2 6.8 copy-start
  7.2 313.9 %reduce-scatter.31.cloned.1.call-start = ((), (), s32[]{:S(2)}) async-start(), calls=%async_computation.13 | async-start | bytes 2506752 | tf_op jit(solution)/shard_map/reduce_scatter | solution.py:205
  38.4 4.6 copy-start.33
  42.9 0.6 copy-start.19
  54.1 3.4 copy-start.11
  57.5 3.7 copy-start.1
  57.5 3.7 copy-start.7
  61.2 2.3 copy-start.18
  63.5 2.3 copy-start.31
  63.5 3.1 copy-start.30
  66.6 3.9 copy-start.34
  66.6 31.2 %slice-start = ((s8[4718592]{0:T(1024)(128)(4,1)}), s8[4194304]{0:T(1024)(128)(4,1)S(1)}, s32[]{:S(2)}) async-start(s8[4718592]{0:T(1024)(128)(4,1)} %bitcast.199), calls=%async_computation.28 | async-start | bytes 8388608
  70.0 27.8 %copy-start.5 = (f32[768,768]{1,0:T(8,128)}, f32[768,768]{1,0:T(8,128)S(1)}, u32[]{:S(2)}) copy-start(f32[768,768]{1,0:T(8,128)S(1)} %get-tuple-element.87) | copy-start | bytes 7077892
  70.4 27.4 %copy-start.29 = (f32[768]{0:T(1024)S(1)}, f32[768]{0:T(1024)}, u32[]{:S(2)}) copy-start(f32[768]{0:T(1024)} %reduce.8) | copy-start | bytes 9220
  70.4 27.4 %slice-start.1 = ((s8[4718592]{0:T(1024)(128)(4,1)}), s8[524288]{0:T(1024)(128)(4,1)S(1)}, s32[]{:S(2)}) async-start(s8[4718592]{0:T(1024)(128)(4,1)} %bitcast.199), calls=%async_computation.29 | async-start | bytes 1048576
  97.8 4.1 copy-start.36
  97.8 4.6 copy-start.16
  97.8 4.6 copy-start.24
  101.9 2.0 copy-start.2
  101.9 2.0 copy-start.15
  102.4 1.6 copy-start.20
  102.4 1.5 copy-start.17
  134.7 9.6 collective-permute-start
  152.1 3.0 copy-start.3
  155.1 2.2 copy-start.4
  159.7 3.6 copy-start.35
  159.7 14.5 slice-start.2
  163.3 10.9 copy-start.10
  163.3 10.9 copy-start.6
  163.3 10.9 slice-start.3
  174.2 5.1 copy-start.8
  179.3 3.0 copy-start.12
  180.8 1.5 copy-start.9
  184.8 1366.2 %reduce-scatter.33.cloned.1.call-start = ((), (), s32[]{:S(2)}) async-start(), calls=%async_computation.15 | async-start | bytes 10027008 | tf_op jit(solution)/shard_map/reduce_scatter | solution.py:209
  196.3 1356.7 %reduce-scatter.35.cloned.1.call-start = ((), (), s32[]{:S(2)}) async-start(), calls=%async_computation.17 | async-start | bytes 10027008 | tf_op jit(solution)/shard_map/reduce_scatter | solution.py:211
  207.2 1356.3 %reduce-scatter.37.cloned.1.call-start = ((), (), s32[]{:S(2)}) async-start(), calls=%async_computation.19 | async-start | bytes 417792
  264.9 7.5 copy-start.13
  264.9 7.5 copy-start.14
  275.6 6.3 copy-start.22
  275.6 8.3 copy-start.21
  275.7 1289.2 %reduce-scatter.39.cloned.1.call-start = ((), (), s32[]{:S(2)}) async-start(), calls=%async_computation.20 | async-start | bytes 417792
  276.8 6.1 copy-start.23
  276.8 8.2 copy-start.32
  276.9 1289.3 %reduce-scatter.41.cloned.1.call-start = ((), (), s32[]{:S(2)}) async-start(), calls=%async_computation.21 | async-start | bytes 417792
  278.5 1289.0 %reduce-scatter.43.cloned.1.call-start = ((), (), s32[]{:S(2)}) async-start(), calls=%async_computation.22 | async-start | bytes 417792
  280.2 1288.6 %reduce-scatter.45.cloned.1.call-start = ((), (), s32[]{:S(2)}) async-start(), calls=%async_computation.23 | async-start | bytes 417792
  281.9 1288.3 %reduce-scatter.49.cloned.1.call-start = ((), (), s32[]{:S(2)}) async-start(), calls=%async_computation.25 | async-start | bytes 417792
  282.9 1288.7 %reduce-scatter.51.cloned.1.call-start = ((), (), s32[]{:S(2)}) async-start(), calls=%async_computation.26 | async-start | bytes 417792
  283.9 1289.0 %reduce-scatter.53.cloned.1.call-start = ((), (), s32[]{:S(2)}) async-start(), calls=%async_computation.27 | async-start | bytes 417792
  284.9 1299.4 %reduce-scatter.47.cloned.1.call-start = ((), (), s32[]{:S(2)}) async-start(), calls=%async_computation.24 | async-start | bytes 1671168
  291.6 2.8 copy-start.25
  296.2 1370.4 %all-gather.8.cloned.1.call-start = ((), (), s32[]{:S(2)}) async-start(), calls=%async_computation.14 | async-start | bytes 1253376 | tf_op jit(solution)/shard_map/all_gather | solution.py:226
  322.7 1346.7 %all-gather.6.cloned.1.call-start = ((), (), s32[]{:S(2)}) async-start(), calls=%async_computation.12 | async-start | bytes 3760128 | tf_op jit(solution)/shard_map/all_gather | solution.py:217
  1551.0 124.0 %all-gather.10.cloned.1.call-start = ((), (), s32[]{:S(2)}) async-start(), calls=%async_computation.16 | async-start | bytes 5013504 | tf_op jit(solution)/shard_map/all_gather | solution.py:238
  1552.9 163.0 %all-gather.12.cloned.1.call-start = ((), (), s32[]{:S(2)}) async-start(), calls=%async_computation.18 | async-start | bytes 5013504 | tf_op jit(solution)/shard_map/all_gather | solution.py:244
  1575.9 11.1 copy-start.26
  1576.8 10.3 copy-start.27
  1577.6 5.8 copy-start.28
Sparse Core Ops, SparseCore 0:
  185.0 60.2 reduce-scatter.30
  249.9 156.7 reduce-scatter.32
  410.8 160.8 reduce-scatter.34
  575.5 72.8 reduce-scatter.36
  651.7 107.8 reduce-scatter.38
  763.4 66.3 reduce-scatter.40
  833.3 59.6 reduce-scatter.42
  896.9 57.3 reduce-scatter.44
  957.8 81.5 reduce-scatter.48
  1043.1 63.5 reduce-scatter.50
  1110.2 61.8 reduce-scatter.52
  1176.7 66.3 reduce-scatter.46
  1245.4 69.4 all-gather.7
  1551.1 54.9 all-gather.5
  1608.8 52.6 all-gather.9
  1663.7 52.1 all-gather.11
where the time goes:
time: 1750 us; the launch traced here: 1730 us
  blocking collectives  1320 us (75%)
  matrix products  166 us (9%)
  local copies, waits for them, and re-layouts  121 us (7%)
  other arithmetic  60.5 us (3%)
  waiting for transfers between devices  41.9 us (2%)
  between operations  18.7 us (1%)
    unnamed x2, blocking collectives  1290 us
    unnamed x125, local copies, waits for them, and re-layouts  52.3 us
    dot_general x4, matrix products, product(): return jnp.dot(left, right, preferred_element_type=jnp.float32)  40.7 us
  transfers between devices with their start and end apart: 17, of which 2 were waited for; matrix products, arithmetic and copies ran while one was open for 12% of the time, Pallas kernels for 0%

commit v1 on v0

--- a/solution.py
+++ b/solution.py
@@ -1,8 +1,13 @@
+import functools
+
 import jax
 import jax.numpy as jnp
 from jax import lax
+from jax.experimental import pallas as pl
+from jax.experimental.pallas import tpu as pltpu
 from jax.sharding import PartitionSpec as P
 
+OWNERS = 16
 H = 12
 DOCS = 4
 
@@ -274,6 +279,990 @@
     )
 
 
+PAD = 16
+BF = jnp.bfloat16
+F32 = jnp.float32
+MESH = pl.DeviceIdType.MESH
+NEG = -1e30
+ROOT_HALF = 0.7071067811865476
+PEAK = 0.3989422804014327
+
+
+def nn(left, right):
+    return jnp.dot(left, right, preferred_element_type=F32)
+
+
+def nt(left, right):
+    return lax.dot_general(left, right, (((1,), (1,)), ((), ())), preferred_element_type=F32)
+
+
+def tn(left, right):
+    return lax.dot_general(left, right, (((0,), (0,)), ((), ())), preferred_element_type=F32)
+
+
+def iota(shape, dim):
+    return lax.broadcasted_iota(jnp.int32, shape, dim)
+
+
+def gelu_parts(inner):
+    cdf = 0.5 * (1.0 + lax.erf(inner * ROOT_HALF))
+    return cdf, jnp.exp(-0.5 * inner * inner) * PEAK
+
+
+def chunk(index, size):
+    return pl.ds(pl.multiple_of(index * size, size), size)
+
+
+def loop(count, body):
+    def step(index, carry):
+        body(index)
+        return carry
+
+    lax.fori_loop(0, count, step, 0)
+
+
+def main_kernel(
+    n,
+    starts,
+    positives,
+    x_hbm,
+    qkv_hbm,
+    q_bias,
+    v_bias,
+    out_hbm,
+    o_bias,
+    gain1,
+    shift1,
+    up_hbm,
+    u_bias,
+    down_hbm,
+    d_bias,
+    gain2,
+    shift2,
+    hidden_out,
+    hidden_grad,
+    xcls_o,
+    mixed_o,
+    normed_o,
+    act_o,
+    douter_o,
+    dinner_o,
+    datt_o,
+    dq_o,
+    kv_o,
+    vecs,
+    up_sum,
+    x,
+    w_qkv,
+    w_out,
+    w_up,
+    w_down,
+    kv,
+    q,
+    mix,
+    seg_bias,
+    qbd,
+    dbd,
+    probs,
+    p_low,
+    ds_low,
+    spread,
+    xcls,
+    mixed,
+    cls,
+    normed,
+    norm1,
+    inv1,
+    norm2,
+    inv2,
+    act,
+    slope,
+    dinner,
+    douter,
+    datt,
+    dmix,
+    d_cls,
+    dfirst,
+    acc,
+    turned,
+    recv,
+    piece,
+    dq_own,
+    normed_t,
+    low_t,
+    acc_t,
+    hout,
+    hgrad,
+    load_sem,
+    save_sem,
+    xs_sem,
+    xr_sem,
+    ms_sem,
+    mr_sem,
+    vs_sem,
+    ks_sem,
+    pr_sem,
+    cs_sem,
+    cr_sem,
+    qs_sem,
+    qr_sem,
+    gs_sem,
+    gr_sem,
+):
+    enc = lax.axis_index("enc")
+    me = lax.axis_index("dp")
+    other = 1 - enc
+    core = lax.rem(me, 2)
+    sibling = me + 1 - 2 * core
+    width = x.shape[1]
+    tokens = x.shape[0]
+    ff = w_up.shape[1]
+    wide = n * PAD
+    rows = starts.shape[0] // DOCS
+    length = tokens // rows
+    local = rows * DOCS
+    head = width // H
+    pairs = H // 2
+    head_scale = head ** (-0.5)
+    group_cols = width // 4
+    half_feats = width // 2
+    group_rows = H // 4 * PAD
+
+    loads = [
+        pltpu.make_async_copy(x_hbm, x, load_sem.at[0]),
+        pltpu.make_async_copy(
+            qkv_hbm.at[:, pl.ds(width, 2 * width)], w_qkv.at[:, pl.ds(width, 2 * width)], load_sem.at[1]
+        ),
+        pltpu.make_async_copy(
+            qkv_hbm.at[:, pl.ds(0, width)], w_qkv.at[:, pl.ds(0, width)], load_sem.at[2]
+        ),
+        pltpu.make_async_copy(out_hbm, w_out, load_sem.at[3]),
+        pltpu.make_async_copy(up_hbm, w_up, load_sem.at[4]),
+        pltpu.make_async_copy(down_hbm, w_down, load_sem.at[5]),
+    ]
+    for copy in loads:
+        copy.start()
+
+    barrier = pltpu.get_barrier_semaphore()
+
+    def greet(j):
+        peer = lax.rem(me + j + 1, n)
+        pl.semaphore_signal(barrier, inc=1, device_id=(enc, peer), device_id_type=MESH)
+
+    loop(n - 1, greet)
+    pl.semaphore_signal(barrier, inc=1, device_id=(other, me), device_id_type=MESH)
+
+    def to_all(source, target, send, receive):
+        def go(j):
+            peer = lax.rem(me + j + 1, n)
+            pltpu.make_async_remote_copy(
+                src_ref=source,
+                dst_ref=target,
+                send_sem=send.at[j],
+                recv_sem=receive.at[me],
+                device_id=(enc, peer),
+                device_id_type=MESH,
+            ).start()
+
+        loop(n - 1, go)
+
+    def from_all(source, target_of, send, receive):
+        def wait(j):
+            peer = lax.rem(me + j + 1, n)
+            copy = pltpu.make_async_remote_copy(
+                src_ref=source,
+                dst_ref=target_of(peer),
+                send_sem=send.at[j],
+                recv_sem=receive.at[peer],
+                device_id=(enc, peer),
+                device_id_type=MESH,
+            )
+            copy.wait_send()
+            copy.wait_recv()
+
+        loop(n - 1, wait)
+
+    first_col = jnp.full((PAD, 1), -1, jnp.int32)
+    seg_col = jnp.full((PAD, 1), -1, jnp.int32)
+    place_col = iota((PAD, 1), 0)
+    segs = []
+    for r in range(rows):
+        place = iota((1, length), 1)
+        count = jnp.zeros((1, length), jnp.int32)
+        for k in range(DOCS):
+            start = starts[r * DOCS + k]
+            count = count + (place >= start).astype(jnp.int32)
+            order = jnp.int32(0)
+            for m in range(DOCS):
+                order = order + jnp.where(starts[r * DOCS + m] <= start, 1, 0)
+            here = place_col == r * DOCS + k
+            first_col = jnp.where(here, r * length + start, first_col)
+            seg_col = jnp.where(here, r * 8 + order, seg_col)
+        segs.append(count + r * 8)
+    seg_row = jnp.concatenate(segs, axis=1)
+    pick = (iota((PAD, tokens), 1) == first_col).astype(F32).astype(BF)
+    allowed = seg_row == seg_col
+
+    own_rows = pl.ds(pl.multiple_of(me * PAD, PAD), PAD)
+
+    def rows_of(ref):
+        return lambda peer: ref.at[pl.ds(pl.multiple_of(peer * PAD, PAD), PAD)]
+
+    loads[0].wait()
+    xcls[own_rows, :] = nn(pick, x[...]).astype(BF)
+    pl.semaphore_wait(barrier, n)
+    to_all(xcls.at[own_rows], xcls.at[own_rows], xs_sem, xr_sem)
+
+    loads[1].wait()
+
+    def kv_step(j):
+        cols = chunk(j, 256)
+        y = nn(x[...], w_qkv[:, pl.ds(pl.multiple_of(width + j * 256, 256), 256)])
+        kv[:, cols] = y.astype(BF)
+
+    loop(width // 256, kv_step)
+
+    def v_step(j):
+        cols = chunk(j, 256)
+        y = nn(x[...], w_qkv[:, pl.ds(pl.multiple_of(2 * width + j * 256, 256), 256)])
+        kv[:, pl.ds(pl.multiple_of(width + j * 256, 256), 256)] = (y + v_bias[:, cols]).astype(BF)
+
+    loop(width // 256, v_step)
+
+    low_half = iota((1, 128), 1) < head
+
+    def block_diagonal(target, rows16):
+        for p in range(pairs):
+            part = rows16[:, p * 128 : (p + 1) * 128]
+            even = jnp.where(low_half, part, 0.0).astype(BF)
+            odd = jnp.where(low_half, 0.0, part).astype(BF)
+            target[pl.ds(2 * p * PAD, PAD), pl.ds(p * 128, 128)] = even
+            target[pl.ds((2 * p + 1) * PAD, PAD), pl.ds(p * 128, 128)] = odd
+
+    def own_lanes(full):
+        parts = []
+        for p in range(pairs):
+            lanes = slice(p * 128, (p + 1) * 128)
+            even = full[2 * p * PAD : (2 * p + 1) * PAD, lanes]
+            odd = full[(2 * p + 1) * PAD : (2 * p + 2) * PAD, lanes]
+            parts.append(jnp.where(low_half, even, odd))
+        return jnp.concatenate(parts, axis=1)
+
+    loads[2].wait()
+    q_own = (nn(xcls[own_rows, :], w_qkv[:, pl.ds(0, width)]) + q_bias[...]).astype(BF).astype(F32)
+    qbd[...] = jnp.zeros_like(qbd)
+    dbd[...] = jnp.zeros_like(dbd)
+    block_diagonal(qbd, q_own)
+    allowed_all = jnp.concatenate([allowed] * H, axis=0)
+    scores = jnp.where(allowed_all, head_scale * nt(qbd[...], kv[:, pl.ds(0, width)]), NEG)
+    peak = jnp.max(scores, -1, keepdims=True)
+    raw = jnp.where(allowed_all, jnp.exp(scores - peak), 0.0)
+    total = jnp.sum(raw, -1, keepdims=True)
+    weights = raw / jnp.where(total > 0.0, total, 1.0)
+    probs[...] = weights
+    p_low[...] = weights.astype(BF)
+    mixed[own_rows, :] = own_lanes(nn(p_low[...], kv[:, pl.ds(width, width)])).astype(BF)
+    to_all(mixed.at[own_rows], mixed.at[own_rows], ms_sem, mr_sem)
+
+    def send_pieces(side, send, slot):
+        for i in range(8):
+            owner = 2 * i + side
+            source = spread.at[
+                slot,
+                pl.ds((i % 4) * group_rows, group_rows),
+                pl.ds((i // 4) * half_feats, half_feats),
+            ]
+
+            @pl.when(me != owner)
+            def _():
+                pltpu.make_async_remote_copy(
+                    src_ref=source,
+                    dst_ref=recv.at[me],
+                    send_sem=send.at[i],
+                    recv_sem=pr_sem.at[me],
+                    device_id=(enc, owner),
+                    device_id_type=MESH,
+                ).start()
+
+            @pl.when(me == owner)
+            def _():
+                recv[me] = source[...]
+
+    def sent_pieces(side, send, slot):
+        for i in range(8):
+            owner = 2 * i + side
+            source = spread.at[
+                slot,
+                pl.ds((i % 4) * group_rows, group_rows),
+                pl.ds((i // 4) * half_feats, half_feats),
+            ]
+
+            @pl.when(me != owner)
+            def _():
+                pltpu.make_async_remote_copy(
+                    src_ref=source,
+                    dst_ref=recv.at[me],
+                    send_sem=send.at[i],
+                    recv_sem=pr_sem.at[me],
+                    device_id=(enc, owner),
+                    device_id_type=MESH,
+                ).wait_send()
+
+    spread[0] = nn(p_low[...], x[...]).astype(BF)
+    send_pieces(1, vs_sem, 0)
+
+    def q_step(j):
+        cols = chunk(j, 256)
+        y = nn(x[...], w_qkv[:, cols]) + q_bias[:, cols]
+        q[:, cols] = (y.astype(BF).astype(F32) * head_scale).astype(BF)
+
+    loop(width // 256, q_step)
+
+    def attend_row(r):
+        place0 = iota((length, 1), 0)
+        place1 = iota((1, length), 1)
+        count0 = jnp.zeros((length, 1), jnp.int32)
+        count1 = jnp.zeros((1, length), jnp.int32)
+        for k in range(DOCS):
+            start = starts[r * DOCS + k]
+            count0 = count0 + (place0 >= start).astype(jnp.int32)
+            count1 = count1 + (place1 >= start).astype(jnp.int32)
+        seg_bias[...] = jnp.where(count0 == count1, 0.0, NEG)
+        these = chunk(r, length)
+        mask_even = jnp.where(low_half, 1.0, 0.0).astype(BF)
+        mask_odd = jnp.where(low_half, 0.0, 1.0).astype(BF)
+
+        def attend_pair(p):
+            lanes = chunk(p, 128)
+            query = q[these, lanes]
+            key = kv[these, lanes]
+            value = kv[these, pl.ds(pl.multiple_of(width + p * 128, 128), 128)]
+            ext = jnp.concatenate([value, jnp.ones_like(value)], axis=1)
+            outs = []
+            for mask in (mask_even, mask_odd):
+                s = nt(query * mask, key) + seg_bias[...]
+                e = jnp.exp(s - jnp.max(s, -1, keepdims=True)).astype(BF)
+                outs.append(nn(e, ext))
+            even, odd = outs
+            top = jnp.where(low_half, even[:, :128], odd[:, :128])
+            low = jnp.where(low_half, even[:, 128:], odd[:, 128:])
+            mix[these, lanes] = (top / low).astype(BF)
+
+        loop(pairs, attend_pair)
+
+    loop(rows, attend_row)
+
+    def saver(source, target, index):
+        return pltpu.make_async_copy(source, target, save_sem.at[index])
+
+    saves = []
+
+    def save(source, target, index):
+        copy = saver(source, target, index)
+        copy.start()
+        saves.append(copy)
+
+    from_all(xcls.at[own_rows], rows_of(xcls), xs_sem, xr_sem)
+    save(xcls, xcls_o, 0)
+    from_all(mixed.at[own_rows], rows_of(mixed), ms_sem, mr_sem)
+    save(mixed, mixed_o, 1)
+    loads[3].wait()
+
+    def out_step(j):
+        cols = chunk(j, 256)
+        acc[:, cols] = nn(mixed[...], w_out[:, cols]) + o_bias[:, cols] + xcls[:, cols].astype(F32)
+
+    loop(width // 256, out_step)
+
+    def stats(h):
+        centred = h - jnp.mean(h, -1, keepdims=True)
+        inverse = lax.rsqrt(jnp.mean(centred * centred, -1, keepdims=True) + EPS_NORM)
+        return centred * inverse, inverse
+
+    unit, inverse = stats(acc[...])
+    norm1[...] = unit
+    inv1[...] = jnp.broadcast_to(inverse, inv1.shape)
+    level = unit * gain1[...] + shift1[...]
+    normed[...] = level
+    low_t[...] = level.astype(BF)
+    loads[4].wait()
+    loads[5].wait()
+    acc[...] = level + d_bias[...]
+
+    def ff_step(j):
+        cols = chunk(j, 512)
+        inner = nn(low_t[...], w_up[:, cols]) + u_bias[:, cols]
+        cdf, pdf = gelu_parts(inner)
+        slope[:, cols] = cdf + inner * pdf
+        active = (inner * cdf).astype(BF)
+        act[:, cols] = active
+        acc[...] += nn(active, w_down[cols, :])
+
+    loop(ff // 512, ff_step)
+    normed_keep = saver(low_t, normed_o, 2)
+    normed_keep.start()
+    save(act, act_o, 3)
+    unit, inverse = stats(acc[...])
+    norm2[...] = unit
+    inv2[...] = jnp.broadcast_to(inverse, inv2.shape)
+    cls[enc] = (unit * gain2[...] + shift2[...]).astype(BF)
+    half = wide // 2
+    mine = pl.ds(pl.multiple_of(core * half, half), half)
+    theirs = pl.ds(pl.multiple_of((1 - core) * half, half), half)
+    cross = pltpu.make_async_remote_copy(
+        src_ref=cls.at[enc, mine],
+        dst_ref=cls.at[enc, mine],
+        send_sem=cs_sem.at[0],
+        recv_sem=cr_sem.at[0],
+        device_id=(other, me),
+        device_id_type=MESH,
+    )
+    cross.start()
+    cross_in = pltpu.make_async_remote_copy(
+        src_ref=cls.at[enc, mine],
+        dst_ref=cls.at[other, mine],
+        send_sem=cs_sem.at[0],
+        recv_sem=cr_sem.at[0],
+        device_id=(other, me),
+        device_id_type=MESH,
+    )
+    pass_on = pltpu.make_async_remote_copy(
+        src_ref=cls.at[other, mine],
+        dst_ref=cls.at[other, mine],
+        send_sem=cs_sem.at[1],
+        recv_sem=cr_sem.at[1],
+        device_id=(enc, sibling),
+        device_id_type=MESH,
+    )
+    pass_in = pltpu.make_async_remote_copy(
+        src_ref=cls.at[other, mine],
+        dst_ref=cls.at[other, theirs],
+        send_sem=cs_sem.at[1],
+        recv_sem=cr_sem.at[1],
+        device_id=(enc, sibling),
+        device_id_type=MESH,
+    )
+
+    place_row = iota((1, wide), 1)
+
+    def place_step(device, row):
+        for k in range(local):
+            target = positives[device * local + k]
+            padded = target + (PAD - local) * lax.div(target, local)
+            row = jnp.where(place_row == device * PAD + k, padded, row)
+        return row
+
+    pos_row = lax.fori_loop(0, n, place_step, jnp.full((1, wide), -1, jnp.int32))
+
+    @pl.when(core == 0)
+    def _():
+        for j in range(width // 256):
+            cols = pl.ds(j * 256, 256)
+            y = (nn(xcls[...], w_qkv[:, cols]) + q_bias[:, cols]).astype(BF).astype(F32)
+            turned[pl.ds(j * 256, 256), :] = y.T.astype(BF)
+
+    normed_keep.wait()
+
+    def layer_tile(r):
+        these = chunk(r, length)
+
+        def tile_out(j):
+            cols = chunk(j, 256)
+            y = nn(mix[these, :], w_out[:, cols]) + o_bias[:, cols]
+            acc_t[:, cols] = y + x[these, cols].astype(F32)
+
+        loop(width // 256, tile_out)
+        unit, _ = stats(acc_t[...])
+        level = unit * gain1[...] + shift1[...]
+        normed_t[...] = level
+        low_t[...] = level.astype(BF)
+        acc_t[...] = level + d_bias[...]
+
+        def tile_ff(j):
+            cols = chunk(j, 512)
+            inner = nn(low_t[...], w_up[:, cols]) + u_bias[:, cols]
+            active = 0.5 * inner * (1.0 + lax.erf(inner * ROOT_HALF))
+            acc_t[...] += nn(active.astype(BF), w_down[cols, :])
+
+        loop(ff // 512, tile_ff)
+        unit, _ = stats(acc_t[...])
+        hout[these, :] = (unit * gain2[...] + shift2[...]).astype(BF)
+
+    def save_tile(r):
+        these = pl.ds(r * length, length)
+        save(hout.at[these], hidden_out.at[these], 8 + r)
+
+    layer_tile(0)
+    save_tile(0)
+
+    cross.wait_send()
+    cross_in.wait_recv()
+    pass_on.start()
+    pass_on.wait_send()
+    pass_in.wait_recv()
+
+    sim_scale = width ** (-0.5)
+    good_col = lax.rem(iota((wide, 1), 0), PAD) < local
+    good_row = lax.rem(iota((1, wide), 1), PAD) < local
+    raw_sims = sim_scale * nt(cls[1], cls[0])
+    sims = jnp.where(good_col, raw_sims, NEG)
+    sim_peak = jnp.max(sims, 0, keepdims=True)
+    sim_total = sim_peak + jnp.log(jnp.sum(jnp.exp(sims - sim_peak), 0, keepdims=True))
+    target = (iota((wide, wide), 0) == pos_row).astype(F32)
+    losses = sim_total - jnp.sum(raw_sims * target, 0, keepdims=True)
+    loss = jnp.sum(jnp.where(good_row, losses, 0.0), -1, keepdims=True) / (local * n)
+    d_sims = sim_scale * (jnp.exp(sims - sim_total) - target) / local
+    d_sims = jnp.where(good_row, d_sims, 0.0).astype(BF)
+
+    @pl.when(enc == 0)
+    def _():
+        d_cls[...] = tn(d_sims, cls[1])
+
+    @pl.when(enc == 1)
+    def _():
+        d_cls[...] = nn(d_sims, cls[0])
+
+    def column_sum(value):
+        return jnp.sum(value, 0, keepdims=True)
+
+    def back(upstream, unit, inverse, gain):
+        scaled = upstream * gain
+        return inverse[:, :1] * (
+            scaled
+            - jnp.mean(scaled, -1, keepdims=True)
+            - unit * jnp.mean(scaled * unit, -1, keepdims=True)
+        )
+
+    vecs[pl.ds(0, 1), :] = column_sum(d_cls[...] * norm2[...])
+    vecs[pl.ds(1, 1), :] = column_sum(d_cls[...])
+    d_second = back(d_cls[...], norm2[...], inv2[...], gain2[...])
+    acc[...] = d_second
+    d_outer = d_second.astype(BF)
+    douter[...] = d_outer
+    save(douter, douter_o, 4)
+    vecs[pl.ds(2, 1), :] = column_sum(d_outer.astype(F32))
+
+    def ff_back(j):
+        cols = chunk(j, 512)
+        d_active = nt(douter[...], w_down[cols, :])
+        d_low = (d_active * slope[:, cols]).astype(BF)
+        dinner[:, cols] = d_low
+        up_sum[:, cols] = column_sum(d_low.astype(F32))
+        acc[...] += nt(d_low, w_up[:, cols])
+
+    loop(ff // 512, ff_back)
+    save(dinner, dinner_o, 5)
+    vecs[pl.ds(3, 1), :] = column_sum(acc[...] * norm1[...])
+    vecs[pl.ds(4, 1), :] = column_sum(acc[...])
+    d_first = back(acc[...], norm1[...], inv1[...], gain1[...])
+    dfirst[...] = d_first
+    d_low = d_first.astype(BF)
+    datt[...] = d_low
+    save(datt, datt_o, 6)
+    vecs[pl.ds(5, 1), :] = column_sum(d_low.astype(F32))
+
+    def mix_back(j):
+        cols = chunk(j, 256)
+        dmix[:, cols] = nt(datt[...], w_out[cols, :]).astype(BF)
+
+    loop(width // 256, mix_back)
+    vecs[pl.ds(6, 1), :] = column_sum(dmix[...].astype(F32))
+    vecs[pl.ds(7, 1), :] = jnp.broadcast_to(loss, (1, width))
+
+    which = lax.div(me, 2)
+    group = lax.rem(which, 4)
+    part = lax.div(which, 4)
+    piece_cols = pl.ds(pl.multiple_of(group * group_cols, group_cols), group_cols)
+    piece_feats = pl.ds(pl.multiple_of(part * half_feats, half_feats), half_feats)
+
+    def sum_pieces():
+        def wait(j):
+            peer = lax.rem(me + j + 1, n)
+            pltpu.make_async_remote_copy(
+                src_ref=recv.at[peer],
+                dst_ref=recv.at[peer],
+                send_sem=vs_sem.at[0],
+                recv_sem=pr_sem.at[peer],
+                device_id=(enc, peer),
+                device_id_type=MESH,
+            ).wait_recv()
+
+        loop(n - 1, wait)
+        for a in range(H // 4):
+            right = recv[:, pl.ds(a * PAD, PAD), :].reshape(wide, half_feats)
+            left = turned[pl.ds(pl.multiple_of(group * group_cols + a * head, head), head), :]
+            piece[pl.ds(a * head, head), :] = nn(left, right).astype(BF)
+        target = kv_o.at[core, piece_cols, piece_feats]
+        to_all(piece, target, gs_sem, gr_sem)
+        saver(piece, target, 7).start()
+
+    @pl.when(core == 1)
+    def _():
+        for j in range(width // 256):
+            cols = pl.ds(j * 256, 256)
+            turned[pl.ds(j * 256, 256), :] = dmix[:, cols].astype(F32).T.astype(BF)
+        sum_pieces()
+
+    d_own = dmix[own_rows, :].astype(F32)
+    block_diagonal(dbd, d_own)
+    d_weights = nt(dbd[...], kv[:, pl.ds(width, width)])
+    weights = probs[...]
+    inner_sum = jnp.sum(d_weights * weights, -1, keepdims=True)
+    ds_low[...] = (head_scale * weights * (d_weights - inner_sum)).astype(BF)
+    spread[1] = nn(ds_low[...], x[...]).astype(BF)
+    send_pieces(0, ks_sem, 1)
+    d_query = own_lanes(nn(ds_low[...], kv[:, pl.ds(0, width)])).astype(BF)
+    dq_own[...] = d_query
+    to_all(dq_own, dq_o.at[own_rows], qs_sem, qr_sem)
+    save(dq_own, dq_o.at[own_rows], 11)
+
+    layer_tile(1)
+    save_tile(1)
+
+    @pl.when(core == 0)
+    def _():
+        sum_pieces()
+
+    layer_tile(2)
+    save_tile(2)
+
+    spread_q = nt(qbd[...], w_qkv[:, pl.ds(width, width)]).astype(BF)
+    spread_v = nt(dbd[...], w_qkv[:, pl.ds(2 * width, width)]).astype(BF)
+    base = dfirst[own_rows, :] + nt(dq_own[...], w_qkv[:, pl.ds(0, width)])
+    base = base.astype(BF)
+    for r in range(rows):
+        these = slice(r * length, (r + 1) * length)
+        y = tn(ds_low[:, these], spread_q) + tn(p_low[:, these], spread_v) + tn(pick[:, these], base)
+        hgrad[pl.ds(r * length, length), :] = y.astype(BF)
+    save(hgrad, hidden_grad, 12)
+
+    sent_pieces(1, vs_sem, 0)
+    sent_pieces(0, ks_sem, 1)
+    from_all(dq_own, rows_of(dq_o), qs_sem, qr_sem)
+
+    def grad_of(peer):
+        other_which = lax.div(peer, 2)
+        return kv_o.at[
+            lax.rem(peer, 2),
+            pl.ds(pl.multiple_of(lax.rem(other_which, 4) * group_cols, group_cols), group_cols),
+            pl.ds(pl.multiple_of(lax.div(other_which, 4) * half_feats, half_feats), half_feats),
+        ]
+
+    from_all(piece, grad_of, gs_sem, gr_sem)
+    saver(piece, kv_o.at[core, piece_cols, piece_feats], 7).wait()
+    for copy in saves:
+        copy.wait()
+
+
+def grad_kernel(
+    xcls_i,
+    mixed_i,
+    normed_i,
+    act_i,
+    douter_i,
+    dinner_i,
+    datt_i,
+    dq_i,
+    kv_i,
+    hidden_out_i,
+    hidden_grad_i,
+    vecs,
+    up_sum,
+    loss,
+    hidden_out,
+    hidden_grad,
+    grad_qkv,
+    grad_query_bias,
+    grad_value_bias,
+    grad_out,
+    grad_out_bias,
+    grad_first_gain,
+    grad_first_shift,
+    grad_up,
+    grad_up_bias,
+    grad_down,
+    grad_down_bias,
+    grad_second_gain,
+    grad_second_shift,
+    xcls,
+    mixed,
+    normed,
+    act,
+    douter,
+    dinner,
+    datt,
+    dq,
+    kv,
+    g_qkv,
+    g_out,
+    g_up,
+    g_down,
+    in_sem,
+    out_sem,
+):
+    width = xcls.shape[1]
+    ff = act.shape[1]
+    pairs = [
+        (act_i, act),
+        (douter_i, douter),
+        (normed_i, normed),
+        (dinner_i, dinner),
+        (mixed_i, mixed),
+        (datt_i, datt),
+        (xcls_i, xcls),
+        (dq_i, dq),
+        (kv_i, kv),
+    ]
+    ins = [pltpu.make_async_copy(a, b, in_sem.at[i]) for i, (a, b) in enumerate(pairs)]
+    for copy in ins:
+        copy.start()
+    through = [
+        pltpu.make_async_copy(hidden_out_i, hidden_out, out_sem.at[0]),
+        pltpu.make_async_copy(hidden_grad_i, hidden_grad, out_sem.at[1]),
+    ]
+    for copy in through:
+        copy.start()
+
+    loss[...] = vecs[pl.ds(7, 1), pl.ds(0, 1)]
+    grad_second_gain[...] = vecs[pl.ds(0, 1), :]
+    grad_second_shift[...] = vecs[pl.ds(1, 1), :]
+    grad_down_bias[...] = vecs[pl.ds(2, 1), :]
+    grad_first_gain[...] = vecs[pl.ds(3, 1), :]
+    grad_first_shift[...] = vecs[pl.ds(4, 1), :]
+    grad_out_bias[...] = vecs[pl.ds(5, 1), :]
+    grad_value_bias[...] = vecs[pl.ds(6, 1), :]
+    grad_up_bias[...] = up_sum[...]
+
+    ins[0].wait()
+    ins[1].wait()
+
+    def down_step(j):
+        these = chunk(j, 256)
+        g_down[these, :] = tn(act[:, these], douter[...])
+        pltpu.make_async_copy(g_down.at[these], grad_down.at[0, these], out_sem.at[2]).start()
+
+    loop(ff // 256, down_step)
+    ins[2].wait()
+    ins[3].wait()
+
+    def up_step(j):
+        these = chunk(j, 128)
+        g_up[these, :] = tn(normed[:, these], dinner[...])
+        pltpu.make_async_copy(g_up.at[these], grad_up.at[0, these], out_sem.at[3]).start()
+
+    loop(width // 128, up_step)
+    ins[4].wait()
+    ins[5].wait()
+
+    def out_step(j):
+        these = chunk(j, 128)
+        g_out[these, :] = tn(mixed[:, these], datt[...])
+        pltpu.make_async_copy(g_out.at[these], grad_out.at[0, these], out_sem.at[4]).start()
+
+    loop(width // 128, out_step)
+    ins[6].wait()
+    ins[7].wait()
+    ins[8].wait()
+    grad_query_bias[...] = jnp.sum(dq[...].astype(F32), 0, keepdims=True)
+
+    def qkv_step(j):
+        these = chunk(j, 128)
+        g_qkv[these, pl.ds(0, width)] = tn(xcls[:, these], dq[...])
+        for m in range(2):
+            g_qkv[these, pl.ds((m + 1) * width, width)] = kv[m, :, these].astype(F32).T
+        pltpu.make_async_copy(g_qkv.at[these], grad_qkv.at[0, these], out_sem.at[5]).start()
+
+    loop(width // 128, qkv_step)
+    pltpu.make_async_copy(g_down, grad_down.at[0], out_sem.at[2]).wait()
+    pltpu.make_async_copy(g_up, grad_up.at[0], out_sem.at[3]).wait()
+    pltpu.make_async_copy(g_out, grad_out.at[0], out_sem.at[4]).wait()
+    pltpu.make_async_copy(g_qkv, grad_qkv.at[0], out_sem.at[5]).wait()
+    for copy in through:
+        copy.wait()
+
+
+def fused_on_device(n, *args):
+    (
+        hidden_in,
+        starts,
+        positives,
+        qkv_weight,
+        query_bias,
+        value_bias,
+        out_weight,
+        out_bias,
+        first_gain,
+        first_shift,
+        up_weight,
+        up_bias,
+        down_weight,
+        down_bias,
+        second_gain,
+        second_shift,
+    ) = args
+    rows, length, width = hidden_in.shape[1:]
+    tokens = rows * length
+    ff = up_weight.shape[-1]
+    wide = n * PAD
+    spreads = H * PAD
+    shape = jax.ShapeDtypeStruct
+    hbm = pl.BlockSpec(memory_space=pl.ANY)
+    vmem = pl.BlockSpec(memory_space=pltpu.VMEM)
+    smem = pl.BlockSpec(memory_space=pltpu.SMEM)
+    dma = pltpu.SemaphoreType.DMA
+    limit = 60 * 1024 * 1024
+    outs = pl.pallas_call(
+        functools.partial(main_kernel, n),
+        out_shape=[
+            shape((tokens, width), BF),
+            shape((tokens, width), BF),
+            shape((wide, width), BF),
+            shape((wide, width), BF),
+            shape((wide, width), BF),
+            shape((wide, ff), BF),
+            shape((wide, width), BF),
+            shape((wide, ff), BF),
+            shape((wide, width), BF),
+            shape((wide, width), BF),
+            shape((2, width, width), BF),
+            shape((8, width), F32),
+            shape((1, ff), F32),
+        ],
+        in_specs=[smem, smem, hbm, hbm, vmem, vmem, hbm, vmem, vmem, vmem, hbm, vmem, hbm, vmem, vmem, vmem],
+        out_specs=[hbm] * 11 + [vmem] * 2,
+        scratch_shapes=[
+            pltpu.VMEM((tokens, width), BF),
+            pltpu.VMEM((width, 3 * width), BF),
+            pltpu.VMEM((width, width), BF),
+            pltpu.VMEM((width, ff), BF),
+            pltpu.VMEM((ff, width), BF),
+            pltpu.VMEM((tokens, 2 * width), BF),
+            pltpu.VMEM((tokens, width), BF),
+            pltpu.VMEM((tokens, width), BF),
+            pltpu.VMEM((length, length), F32),
+            pltpu.VMEM((spreads, width), BF),
+            pltpu.VMEM((spreads, width), BF),
+            pltpu.VMEM((spreads, tokens), F32),
+            pltpu.VMEM((spreads, tokens), BF),
+            pltpu.VMEM((spreads, tokens), BF),
+            pltpu.VMEM((2, spreads, width), BF),
+            pltpu.VMEM((wide, width), BF),
+            pltpu.VMEM((wide, width), BF),
+            pltpu.VMEM((2, wide, width), BF),
+            pltpu.VMEM((wide, width), F32),
+            pltpu.VMEM((wide, width), F32),
+            pltpu.VMEM((wide, 128), F32),
+            pltpu.VMEM((wide, width), F32),
+            pltpu.VMEM((wide, 128), F32),
+            pltpu.VMEM((wide, ff), BF),
+            pltpu.VMEM((wide, ff), F32),
+            pltpu.VMEM((wide, ff), BF),
+            pltpu.VMEM((wide, width), BF),
+            pltpu.VMEM((wide, width), BF),
+            pltpu.VMEM((wide, width), BF),
+            pltpu.VMEM((wide, width), F32),
+            pltpu.VMEM((wide, width), F32),
+            pltpu.VMEM((wide, width), F32),
+            pltpu.VMEM((width, wide), BF),
+            pltpu.VMEM((n, H // 4 * PAD, width // 2), BF),
+            pltpu.VMEM((width // 4, width // 2), BF),
+            pltpu.VMEM((PAD, width), BF),
+            pltpu.VMEM((length, width), F32),
+            pltpu.VMEM((length, width), BF),
+            pltpu.VMEM((length, width), F32),
+            pltpu.VMEM((tokens, width), BF),
+            pltpu.VMEM((tokens, width), BF),
+            dma((6,)),
+            dma((13,)),
+            dma((n,)),
+            dma((n,)),
+            dma((n,)),
+            dma((n,)),
+            dma((8,)),
+            dma((8,)),
+            dma((n,)),
+            dma((2,)),
+            dma((2,)),
+            dma((n,)),
+            dma((n,)),
+            dma((n,)),
+            dma((n,)),
+        ],
+        compiler_params=pltpu.CompilerParams(
+            collective_id=0, has_side_effects=True, vmem_limit_bytes=limit
+        ),
+        name="layer",
+    )(
+        starts.reshape(rows * DOCS),
+        positives,
+        hidden_in.reshape(tokens, width),
+        qkv_weight.reshape(width, 3 * width),
+        query_bias,
+        value_bias,
+        out_weight.reshape(width, width),
+        out_bias,
+        first_gain,
+        first_shift,
+        up_weight.reshape(width, ff),
+        up_bias,
+        down_weight.reshape(ff, width),
+        down_bias,
+        second_gain,
+        second_shift,
+    )
+    (h_out, h_grad, xcls, mixed, normed, act, douter, dinner, datt, dq, kv, vecs, up_sum) = outs
+    row = shape((1, width), F32)
+    grads = pl.pallas_call(
+        grad_kernel,
+        out_shape=[
+            shape((1, 1), F32),
+            shape((tokens, width), BF),
+            shape((tokens, width), BF),
+            shape((1, width, 3 * width), F32),
+            row,
+            row,
+            shape((1, width, width), F32),
+            row,
+            row,
+            row,
+            shape((1, width, ff), F32),
+            shape((1, ff), F32),
+            shape((1, ff, width), F32),
+            row,
+            row,
+            row,
+        ],
+        in_specs=[hbm] * 11 + [vmem] * 2,
+        out_specs=[vmem, hbm, hbm, hbm, vmem, vmem, hbm, vmem, vmem, vmem, hbm, vmem, hbm, vmem, vmem, vmem],
+        scratch_shapes=[
+            pltpu.VMEM((wide, width), BF),
+            pltpu.VMEM((wide, width), BF),
+            pltpu.VMEM((wide, width), BF),
+            pltpu.VMEM((wide, ff), BF),
+            pltpu.VMEM((wide, width), BF),
+            pltpu.VMEM((wide, ff), BF),
+            pltpu.VMEM((wide, width), BF),
+            pltpu.VMEM((wide, width), BF),
+            pltpu.VMEM((2, width, width), BF),
+            pltpu.VMEM((width, 3 * width), F32),
+            pltpu.VMEM((width, width), F32),
+            pltpu.VMEM((width, ff), F32),
+            pltpu.VMEM((ff, width), F32),
+            dma((9,)),
+            dma((6,)),
+        ],
+        compiler_params=pltpu.CompilerParams(vmem_limit_bytes=limit),
+        name="gradients",
+    )(xcls, mixed, normed, act, douter, dinner, datt, dq, kv, h_out, h_grad, vecs, up_sum)
+    block = (1, rows, length, width)
+    return (
+        grads[0].reshape(()),
+        grads[1].reshape(block),
+        grads[2].reshape(block),
+        *grads[3:],
+    )
+
+
 def solution(mesh):
     placed = (
         P("enc", "dp", None, None),
@@ -293,8 +1282,10 @@
         P("enc", None),
         P("enc", None),
     )
+    n = mesh.shape["dp"]
+    body = functools.partial(fused_on_device, n) if n == OWNERS else on_device
     return jax.shard_map(
-        on_device,
+        body,
         mesh=mesh,
         in_specs=placed,
         out_specs=(

time: 1750 us -> 195 us (0.11)
  the two profiles are of different devices: /device:TPU:0 before, /device:TPU:15 now
where the time goes in v1:
time: 195 us
  Pallas kernels  193 us (99%)
    pallas_call x1, Pallas kernels, fused_on_device(): pl.pallas_call(functools.partial(main_kernel, n), out_shape=[shape((token...  119 us
    pallas_call x1, Pallas kernels, fused_on_device(): pl.pallas_call(grad_kernel, out_shape=[shape((1, 1), F32), shape((tokens,...  74.1 us

profile of v1, /device:TPU:15, one launch (start us, length us, event | category | flops | bytes accessed | tf_op | source)
XLA Modules:
  0.0 194.9 jit_solution(17227005217674001331)
XLA Ops:
  0.6 0.7 reduce
  1.3 0.6 reshape.59.starts
  1.9 118.6 %layer.1 = (bf16[768,768]{1,0:T(8,128)(2,1)}, bf16[768,768]{1,0:T(8,128)(2,1)}, bf16[256,768]{1,0:T(8,128)(2,1)}, bf16[256,768]{1,0:T(8,128)(2,1)}, bf16[256,768...) custom-call(s32[12]{0:T(128)} %reshape.59.starts, ...), custom_call_target="tpu_custom_call" | custom-call | tf_op jit(solution)/shard_map/layer/pallas_call | solution.py:1114
  120.6 74.1 %gradients.1 = (f32[1,1]{1,0:T(1,128)}, bf16[768,768]{1,0:T(8,128)(2,1)}, bf16[768,768]{1,0:T(8,128)(2,1)}, f32[1,768,2304]{2,1,0:T(8,128)}, f32[1,768]{1,0:T(1,...) custom-call(bf16[256,768]{1,0:T(8,128)(2,1)} %get-tuple-element.45.x, ...), custom_call_target="tpu_custom_call" | custom-call | tf_op jit(solution)/shard_map/gradients/pallas_call | solution.py:1215

commit v2 on v1

--- a/solution.py
+++ b/solution.py
@@ -452,35 +452,46 @@
     loop(n - 1, greet)
     pl.semaphore_signal(barrier, inc=1, device_id=(other, me), device_id_type=MESH)
 
-    def to_all(source, target, send, receive):
+    def remote(source, target, send, receive, device):
+        return pltpu.make_async_remote_copy(
+            src_ref=source,
+            dst_ref=target,
+            send_sem=send,
+            recv_sem=receive,
+            device_id=device,
+            device_id_type=MESH,
+        )
+
+    def same_core(j):
+        return lax.rem(me + 2 * j + 2, n)
+
+    def share(source, place, send, receive):
         def go(j):
-            peer = lax.rem(me + j + 1, n)
-            pltpu.make_async_remote_copy(
-                src_ref=source,
-                dst_ref=target,
-                send_sem=send.at[j],
-                recv_sem=receive.at[me],
-                device_id=(enc, peer),
-                device_id_type=MESH,
+            remote(source, place(me), send.at[j], receive.at[me], (enc, same_core(j))).start()
+
+        loop(n // 2 - 1, go)
+        remote(source, place(me), send.at[n - 2], receive.at[me], (enc, sibling)).start()
+
+    def shared(source, place, send, receive):
+        def pass_on(j):
+            peer = same_core(j)
+            remote(source, place(peer), send.at[j], receive.at[peer], (enc, peer)).wait_recv()
+            remote(
+                place(peer), place(peer), send.at[n // 2 - 1 + j], receive.at[peer], (enc, sibling)
             ).start()
 
-        loop(n - 1, go)
-
-    def from_all(source, target_of, send, receive):
-        def wait(j):
-            peer = lax.rem(me + j + 1, n)
-            copy = pltpu.make_async_remote_copy(
-                src_ref=source,
-                dst_ref=target_of(peer),
-                send_sem=send.at[j],
-                recv_sem=receive.at[peer],
-                device_id=(enc, peer),
-                device_id_type=MESH,
-            )
-            copy.wait_send()
-            copy.wait_recv()
-
-        loop(n - 1, wait)
+        loop(n // 2 - 1, pass_on)
+
+        def finish(j):
+            peer = lax.rem(same_core(j) + 1 - 2 * core + n, n)
+            remote(source, place(peer), send.at[0], receive.at[peer], (enc, sibling)).wait_recv()
+
+        loop(n // 2, finish)
+
+        def sent(j):
+            remote(source, place(me), send.at[j], receive.at[me], (enc, sibling)).wait_send()
+
+        loop(n - 1, sent)
 
     first_col = jnp.full((PAD, 1), -1, jnp.int32)
     seg_col = jnp.full((PAD, 1), -1, jnp.int32)
@@ -511,7 +522,7 @@
     loads[0].wait()
     xcls[own_rows, :] = nn(pick, x[...]).astype(BF)
     pl.semaphore_wait(barrier, n)
-    to_all(xcls.at[own_rows], xcls.at[own_rows], xs_sem, xr_sem)
+    share(xcls.at[own_rows], rows_of(xcls), xs_sem, xr_sem)
 
     loads[1].wait()
 
@@ -562,7 +573,7 @@
     probs[...] = weights
     p_low[...] = weights.astype(BF)
     mixed[own_rows, :] = own_lanes(nn(p_low[...], kv[:, pl.ds(width, width)])).astype(BF)
-    to_all(mixed.at[own_rows], mixed.at[own_rows], ms_sem, mr_sem)
+    share(mixed.at[own_rows], rows_of(mixed), ms_sem, mr_sem)
 
     def send_pieces(side, send, slot):
         for i in range(8):
@@ -662,9 +673,9 @@
         copy.start()
         saves.append(copy)
 
-    from_all(xcls.at[own_rows], rows_of(xcls), xs_sem, xr_sem)
+    shared(xcls.at[own_rows], rows_of(xcls), xs_sem, xr_sem)
     save(xcls, xcls_o, 0)
-    from_all(mixed.at[own_rows], rows_of(mixed), ms_sem, mr_sem)
+    shared(mixed.at[own_rows], rows_of(mixed), ms_sem, mr_sem)
     save(mixed, mixed_o, 1)
     loads[3].wait()
 
@@ -871,9 +882,23 @@
 
     which = lax.div(me, 2)
     group = lax.rem(which, 4)
-    part = lax.div(which, 4)
-    piece_cols = pl.ds(pl.multiple_of(group * group_cols, group_cols), group_cols)
-    piece_feats = pl.ds(pl.multiple_of(part * half_feats, half_feats), half_feats)
+
+    planes = n // 4
+    across = me + 2 - 4 * lax.rem(which, 2)
+
+    def up_down(j):
+        return lax.rem(me + 4 * j + 4, n)
+
+    def grad_of(peer):
+        index = lax.div(peer, 2)
+        return kv_o.at[
+            lax.rem(peer, 2),
+            pl.ds(pl.multiple_of(lax.rem(index, 4) * group_cols, group_cols), group_cols),
+            pl.ds(pl.multiple_of(lax.div(index, 4) * half_feats, half_feats), half_feats),
+        ]
+
+    def gradient(slot, source, owner, device):
+        return remote(source, grad_of(owner), gs_sem.at[slot], gr_sem.at[owner], (enc, device))
 
     def sum_pieces():
         def wait(j):
@@ -892,9 +917,37 @@
             right = recv[:, pl.ds(a * PAD, PAD), :].reshape(wide, half_feats)
             left = turned[pl.ds(pl.multiple_of(group * group_cols + a * head, head), head), :]
             piece[pl.ds(a * head, head), :] = nn(left, right).astype(BF)
-        target = kv_o.at[core, piece_cols, piece_feats]
-        to_all(piece, target, gs_sem, gr_sem)
-        saver(piece, target, 7).start()
+        for j in range(planes - 1):
+            gradient(j, piece, me, up_down(j)).start()
+        gradient(planes - 1, piece, me, across).start()
+        gradient(planes, piece, me, sibling).start()
+        saver(piece, grad_of(me), 7).start()
+
+    def pass_plane():
+        for j in range(planes - 1):
+            peer = up_down(j)
+            gradient(0, grad_of(peer), peer, peer).wait_recv()
+            gradient(planes + 1 + 2 * j, grad_of(peer), peer, across).start()
+            gradient(planes + 2 + 2 * j, grad_of(peer), peer, sibling).start()
+
+    def pass_across():
+        for j in range(planes):
+            peer = across if j == 0 else lax.rem(up_down(j - 1) - me + across + n, n)
+            gradient(0, grad_of(peer), peer, across).wait_recv()
+            gradient(3 * planes - 1 + j, grad_of(peer), peer, sibling).start()
+
+    def finish_gradients():
+        def came(j):
+            peer = lax.rem(same_core(j) + 1 - 2 * core + n, n)
+            gradient(0, grad_of(peer), peer, sibling).wait_recv()
+
+        loop(n // 2, came)
+
+        def sent(j):
+            remote(piece, grad_of(me), gs_sem.at[j], gr_sem.at[me], (enc, sibling)).wait_send()
+
+        loop(4 * planes - 1, sent)
+        saver(piece, grad_of(me), 7).wait()
 
     @pl.when(core == 1)
     def _():
@@ -913,7 +966,7 @@
     send_pieces(0, ks_sem, 1)
     d_query = own_lanes(nn(ds_low[...], kv[:, pl.ds(0, width)])).astype(BF)
     dq_own[...] = d_query
-    to_all(dq_own, dq_o.at[own_rows], qs_sem, qr_sem)
+    share(dq_own, rows_of(dq_o), qs_sem, qr_sem)
     save(dq_own, dq_o.at[own_rows], 11)
 
     layer_tile(1)
@@ -938,18 +991,11 @@
 
     sent_pieces(1, vs_sem, 0)
     sent_pieces(0, ks_sem, 1)
-    from_all(dq_own, rows_of(dq_o), qs_sem, qr_sem)
-
-    def grad_of(peer):
-        other_which = lax.div(peer, 2)
-        return kv_o.at[
-            lax.rem(peer, 2),
-            pl.ds(pl.multiple_of(lax.rem(other_which, 4) * group_cols, group_cols), group_cols),
-            pl.ds(pl.multiple_of(lax.div(other_which, 4) * half_feats, half_feats), half_feats),
-        ]
-
-    from_all(piece, grad_of, gs_sem, gr_sem)
-    saver(piece, kv_o.at[core, piece_cols, piece_feats], 7).wait()
+    shared(dq_own, rows_of(dq_o), qs_sem, qr_sem)
+
+    pass_plane()
+    pass_across()
+    finish_gradients()
     for copy in saves:
         copy.wait()
 
@@ -997,6 +1043,8 @@
     g_out,
     g_up,
     g_down,
+    h_out,
+    h_grad,
     in_sem,
     out_sem,
 ):
@@ -1016,11 +1064,11 @@
     ins = [pltpu.make_async_copy(a, b, in_sem.at[i]) for i, (a, b) in enumerate(pairs)]
     for copy in ins:
         copy.start()
-    through = [
-        pltpu.make_async_copy(hidden_out_i, hidden_out, out_sem.at[0]),
-        pltpu.make_async_copy(hidden_grad_i, hidden_grad, out_sem.at[1]),
+    through_in = [
+        pltpu.make_async_copy(hidden_out_i, h_out, in_sem.at[9]),
+        pltpu.make_async_copy(hidden_grad_i, h_grad, in_sem.at[10]),
     ]
-    for copy in through:
+    for copy in through_in:
         copy.start()
 
     loss[...] = vecs[pl.ds(7, 1), pl.ds(0, 1)]
@@ -1051,6 +1099,13 @@
         pltpu.make_async_copy(g_up.at[these], grad_up.at[0, these], out_sem.at[3]).start()
 
     loop(width // 128, up_step)
+    through = [
+        pltpu.make_async_copy(h_out, hidden_out, out_sem.at[0]),
+        pltpu.make_async_copy(h_grad, hidden_grad, out_sem.at[1]),
+    ]
+    for came, copy in zip(through_in, through):
+        came.wait()
+        copy.start()
     ins[4].wait()
     ins[5].wait()
 
@@ -1248,7 +1303,9 @@
             pltpu.VMEM((width, width), F32),
             pltpu.VMEM((width, ff), F32),
             pltpu.VMEM((ff, width), F32),
-            dma((9,)),
+            pltpu.VMEM((tokens, width), BF),
+            pltpu.VMEM((tokens, width), BF),
+            dma((11,)),
             dma((6,)),
         ],
         compiler_params=pltpu.CompilerParams(vmem_limit_bytes=limit),

time: 195 us -> 106 us (0.54)
  the two profiles are of different devices: /device:TPU:15 before, /device:TPU:0 now
where the time goes in v2:
time: 106 us
  Pallas kernels  104 us (98%)
    pallas_call x1, Pallas kernels, fused_on_device(): pl.pallas_call(functools.partial(main_kernel, n), out_shape=[shape((token...  89.7 us
    pallas_call x1, Pallas kernels, fused_on_device(): pl.pallas_call(grad_kernel, out_shape=[shape((1, 1), F32), shape((tokens,...  14.2 us

profile of v2, /device:TPU:0, one launch (start us, length us, event | category | flops | bytes accessed | tf_op | source)
XLA Modules:
  0.0 106.0 jit_solution(6417910547781663907)
XLA Ops:
  0.6 0.7 reduce
  1.3 0.6 reshape.59.starts
  1.9 89.7 %layer.1 = (bf16[768,768]{1,0:T(8,128)(2,1)}, bf16[768,768]{1,0:T(8,128)(2,1)}, bf16[256,768]{1,0:T(8,128)(2,1)}, bf16[256,768]{1,0:T(8,128)(2,1)}, bf16[256,768...) custom-call(s32[12]{0:T(128)} %reshape.59.starts, ...), custom_call_target="tpu_custom_call" | custom-call | tf_op jit(solution)/shard_map/layer/pallas_call | solution.py:1169
  91.6 14.2 %gradients.1 = (f32[1,1]{1,0:T(1,128)}, bf16[768,768]{1,0:T(8,128)(2,1)}, bf16[768,768]{1,0:T(8,128)(2,1)}, f32[1,768,2304]{2,1,0:T(8,128)}, f32[1,768]{1,0:T(1,...) custom-call(bf16[256,768]{1,0:T(8,128)(2,1)} %get-tuple-element.45.x, ...), custom_call_target="tpu_custom_call" | custom-call | tf_op jit(solution)/shard_map/gradients/pallas_call | solution.py:1270

commit v3 on v2

--- a/solution.py
+++ b/solution.py
@@ -349,9 +349,8 @@
     dinner_o,
     datt_o,
     dq_o,
+    vecs_o,
     kv_o,
-    vecs,
-    up_sum,
     x,
     w_qkv,
     w_out,
@@ -363,18 +362,21 @@
     seg_bias,
     qbd,
     dbd,
+    qk,
+    dv,
     probs,
     p_low,
     ds_low,
-    spread,
+    px,
+    dx,
     xcls,
     mixed,
     cls,
-    normed,
     norm1,
     inv1,
     norm2,
     inv2,
+    normed,
     act,
     slope,
     dinner,
@@ -384,11 +386,11 @@
     d_cls,
     dfirst,
     acc,
+    vecs,
     turned,
     recv,
     piece,
     dq_own,
-    normed_t,
     low_t,
     acc_t,
     hout,
@@ -399,26 +401,30 @@
     xr_sem,
     ms_sem,
     mr_sem,
-    vs_sem,
     ks_sem,
-    pr_sem,
+    kr_sem,
     cs_sem,
     cr_sem,
     qs_sem,
     qr_sem,
+    vs_sem,
     gs_sem,
     gr_sem,
+    fs_sem,
+    fr_sem,
 ):
     enc = lax.axis_index("enc")
     me = lax.axis_index("dp")
     other = 1 - enc
     core = lax.rem(me, 2)
+    which = lax.div(me, 2)
     sibling = me + 1 - 2 * core
-    width = x.shape[1]
-    tokens = x.shape[0]
+    across = me + 2 - 4 * lax.rem(which, 2)
+    planes = n // 4
+    tokens, width = x.shape
     ff = w_up.shape[1]
-    wide = n * PAD
-    rows = starts.shape[0] // DOCS
+    side = n // 2 * PAD
+    rows = starts.shape[1]
     length = tokens // rows
     local = rows * DOCS
     head = width // H
@@ -427,18 +433,21 @@
     group_cols = width // 4
     half_feats = width // 2
     group_rows = H // 4 * PAD
+    query_w = pl.ds(0, width)
+    key_w = pl.ds(width, width)
+    value_w = pl.ds(2 * width, width)
+
+    def weight_load(cols, index):
+        return pltpu.make_async_copy(qkv_hbm.at[:, cols], w_qkv.at[:, cols], load_sem.at[index])
 
     loads = [
         pltpu.make_async_copy(x_hbm, x, load_sem.at[0]),
-        pltpu.make_async_copy(
-            qkv_hbm.at[:, pl.ds(width, 2 * width)], w_qkv.at[:, pl.ds(width, 2 * width)], load_sem.at[1]
-        ),
-        pltpu.make_async_copy(
-            qkv_hbm.at[:, pl.ds(0, width)], w_qkv.at[:, pl.ds(0, width)], load_sem.at[2]
-        ),
-        pltpu.make_async_copy(out_hbm, w_out, load_sem.at[3]),
-        pltpu.make_async_copy(up_hbm, w_up, load_sem.at[4]),
-        pltpu.make_async_copy(down_hbm, w_down, load_sem.at[5]),
+        weight_load(key_w, 1),
+        weight_load(query_w, 2),
+        weight_load(value_w, 3),
+        pltpu.make_async_copy(out_hbm, w_out, load_sem.at[4]),
+        pltpu.make_async_copy(up_hbm, w_up, load_sem.at[5]),
+        pltpu.make_async_copy(down_hbm, w_down, load_sem.at[6]),
     ]
     for copy in loads:
         copy.start()
@@ -465,33 +474,91 @@
     def same_core(j):
         return lax.rem(me + 2 * j + 2, n)
 
+    def cousin(j):
+        return lax.rem(same_core(j) + 1 - 2 * core + n, n)
+
+    def up_down(j):
+        return lax.rem(me + 4 * j + 4, n)
+
+    def block(index):
+        return pl.ds(pl.multiple_of(index * PAD, PAD), PAD)
+
+    own = block(which)
+
     def share(source, place, send, receive):
         def go(j):
             remote(source, place(me), send.at[j], receive.at[me], (enc, same_core(j))).start()
 
         loop(n // 2 - 1, go)
-        remote(source, place(me), send.at[n - 2], receive.at[me], (enc, sibling)).start()
 
     def shared(source, place, send, receive):
-        def pass_on(j):
+        def came(j):
             peer = same_core(j)
-            remote(source, place(peer), send.at[j], receive.at[peer], (enc, peer)).wait_recv()
-            remote(
-                place(peer), place(peer), send.at[n // 2 - 1 + j], receive.at[peer], (enc, sibling)
-            ).start()
-
-        loop(n // 2 - 1, pass_on)
-
-        def finish(j):
-            peer = lax.rem(same_core(j) + 1 - 2 * core + n, n)
-            remote(source, place(peer), send.at[0], receive.at[peer], (enc, sibling)).wait_recv()
-
-        loop(n // 2, finish)
-
-        def sent(j):
-            remote(source, place(me), send.at[j], receive.at[me], (enc, sibling)).wait_send()
-
-        loop(n - 1, sent)
+            copy = remote(source, place(peer), send.at[j], receive.at[peer], (enc, peer))
+            copy.wait_send()
+            copy.wait_recv()
+
+        loop(n // 2 - 1, came)
+
+    class Relay:
+        def __init__(self, source, place, send, receive):
+            self.source, self.place, self.send, self.receive = source, place, send, receive
+
+        def copy(self, slot, source, owner, device):
+            return remote(
+                source, self.place(owner), self.send.at[slot], self.receive.at[owner], (enc, device)
+            )
+
+        def start(self):
+            for j in range(planes - 1):
+                self.copy(j, self.source, me, up_down(j)).start()
+            self.copy(planes - 1, self.source, me, across).start()
+            self.copy(planes, self.source, me, sibling).start()
+
+        def plane(self):
+            for j in range(planes - 1):
+                peer = up_down(j)
+                self.copy(0, self.place(peer), peer, peer).wait_recv()
+                self.copy(planes + 1 + 2 * j, self.place(peer), peer, across).start()
+                self.copy(planes + 2 + 2 * j, self.place(peer), peer, sibling).start()
+
+        def over(self):
+            for j in range(planes):
+                peer = across if j == 0 else lax.rem(up_down(j - 1) - me + across + n, n)
+                self.copy(0, self.place(peer), peer, across).wait_recv()
+                self.copy(3 * planes - 1 + j, self.place(peer), peer, sibling).start()
+
+        def sent(self):
+            def wait(j):
+                self.copy(j, self.source, me, sibling).wait_send()
+
+            loop(4 * planes - 1, wait)
+
+        def came(self):
+            def wait(j):
+                peer = cousin(j)
+                self.copy(0, self.place(peer), peer, sibling).wait_recv()
+
+            loop(n // 2, wait)
+
+    saves = []
+
+    def save(source, target, index):
+        copy = pltpu.make_async_copy(source, target, save_sem.at[index])
+        copy.start()
+        saves.append(copy)
+
+    halves = [pl.ds(pl.multiple_of(core * side, side), side)]
+    halves.append(pl.ds(pl.multiple_of((1 - core) * side, side), side))
+    given = []
+
+    def give(source, target, index):
+        save(source, target.at[halves[0]], index)
+        copy = remote(source, target.at[halves[0]], fs_sem.at[index], fr_sem.at[index], (enc, sibling))
+        copy.start()
+        given.append(
+            remote(source, target.at[halves[1]], fs_sem.at[index], fr_sem.at[index], (enc, sibling))
+        )
 
     first_col = jnp.full((PAD, 1), -1, jnp.int32)
     seg_col = jnp.full((PAD, 1), -1, jnp.int32)
@@ -501,11 +568,11 @@
         place = iota((1, length), 1)
         count = jnp.zeros((1, length), jnp.int32)
         for k in range(DOCS):
-            start = starts[r * DOCS + k]
+            start = starts[0, r, k]
             count = count + (place >= start).astype(jnp.int32)
             order = jnp.int32(0)
             for m in range(DOCS):
-                order = order + jnp.where(starts[r * DOCS + m] <= start, 1, 0)
+                order = order + jnp.where(starts[0, r, m] <= start, 1, 0)
             here = place_col == r * DOCS + k
             first_col = jnp.where(here, r * length + start, first_col)
             seg_col = jnp.where(here, r * 8 + order, seg_col)
@@ -514,37 +581,11 @@
     pick = (iota((PAD, tokens), 1) == first_col).astype(F32).astype(BF)
     allowed = seg_row == seg_col
 
-    own_rows = pl.ds(pl.multiple_of(me * PAD, PAD), PAD)
-
-    def rows_of(ref):
-        return lambda peer: ref.at[pl.ds(pl.multiple_of(peer * PAD, PAD), PAD)]
-
-    loads[0].wait()
-    xcls[own_rows, :] = nn(pick, x[...]).astype(BF)
-    pl.semaphore_wait(barrier, n)
-    share(xcls.at[own_rows], rows_of(xcls), xs_sem, xr_sem)
-
-    loads[1].wait()
-
-    def kv_step(j):
-        cols = chunk(j, 256)
-        y = nn(x[...], w_qkv[:, pl.ds(pl.multiple_of(width + j * 256, 256), 256)])
-        kv[:, cols] = y.astype(BF)
-
-    loop(width // 256, kv_step)
-
-    def v_step(j):
-        cols = chunk(j, 256)
-        y = nn(x[...], w_qkv[:, pl.ds(pl.multiple_of(2 * width + j * 256, 256), 256)])
-        kv[:, pl.ds(pl.multiple_of(width + j * 256, 256), 256)] = (y + v_bias[:, cols]).astype(BF)
-
-    loop(width // 256, v_step)
-
     low_half = iota((1, 128), 1) < head
 
-    def block_diagonal(target, rows16):
+    def block_diagonal(target, block_rows):
         for p in range(pairs):
-            part = rows16[:, p * 128 : (p + 1) * 128]
+            part = block_rows[:, p * 128 : (p + 1) * 128]
             even = jnp.where(low_half, part, 0.0).astype(BF)
             odd = jnp.where(low_half, 0.0, part).astype(BF)
             target[pl.ds(2 * p * PAD, PAD), pl.ds(p * 128, 128)] = even
@@ -559,11 +600,24 @@
             parts.append(jnp.where(low_half, even, odd))
         return jnp.concatenate(parts, axis=1)
 
-    loads[2].wait()
-    q_own = (nn(xcls[own_rows, :], w_qkv[:, pl.ds(0, width)]) + q_bias[...]).astype(BF).astype(F32)
     qbd[...] = jnp.zeros_like(qbd)
     dbd[...] = jnp.zeros_like(dbd)
+    loads[0].wait()
+    xcls[core, own, :] = nn(pick, x[...]).astype(BF)
+    pl.semaphore_wait(barrier, n)
+
+    def xcls_place(peer):
+        return xcls.at[core, block(lax.div(peer, 2))]
+
+    share(xcls.at[core, own], xcls_place, xs_sem, xr_sem)
+
+    loads[1].wait()
+    kv[:, pl.ds(0, width)] = nn(x[...], w_qkv[:, key_w]).astype(BF)
+    loads[2].wait()
+    q_own = (nn(xcls[core, own, :], w_qkv[:, query_w]) + q_bias[...]).astype(BF).astype(F32)
     block_diagonal(qbd, q_own)
+    loads[3].wait()
+    kv[:, pl.ds(width, width)] = (nn(x[...], w_qkv[:, value_w]) + v_bias[...]).astype(BF)
     allowed_all = jnp.concatenate([allowed] * H, axis=0)
     scores = jnp.where(allowed_all, head_scale * nt(qbd[...], kv[:, pl.ds(0, width)]), NEG)
     peak = jnp.max(scores, -1, keepdims=True)
@@ -572,62 +626,49 @@
     weights = raw / jnp.where(total > 0.0, total, 1.0)
     probs[...] = weights
     p_low[...] = weights.astype(BF)
-    mixed[own_rows, :] = own_lanes(nn(p_low[...], kv[:, pl.ds(width, width)])).astype(BF)
-    share(mixed.at[own_rows], rows_of(mixed), ms_sem, mr_sem)
-
-    def send_pieces(side, send, slot):
-        for i in range(8):
-            owner = 2 * i + side
-            source = spread.at[
-                slot,
-                pl.ds((i % 4) * group_rows, group_rows),
-                pl.ds((i // 4) * half_feats, half_feats),
-            ]
-
-            @pl.when(me != owner)
+    mixed[own, :] = own_lanes(nn(p_low[...], kv[:, pl.ds(width, width)])).astype(BF)
+
+    def mixed_place(peer):
+        return mixed.at[block(lax.div(peer, 2))]
+
+    share(mixed.at[own], mixed_place, ms_sem, mr_sem)
+
+    def slot_of(peer):
+        return lax.rem(peer, 2) * (n // 2) + lax.div(peer, 2)
+
+    def piece_of(source, i):
+        return source.at[
+            pl.ds((i % 4) * group_rows, group_rows), pl.ds((i // 4) * half_feats, half_feats)
+        ]
+
+    def piece_copy(source, side_of, i, send):
+        target = recv.at[slot_of(me)]
+        owner = (enc, 2 * i + side_of)
+        return remote(piece_of(source, i), target, send.at[i], kr_sem.at[me], owner)
+
+    def send_pieces(source, side_of, send):
+        for i in range(n // 2):
+
+            @pl.when(me != 2 * i + side_of)
             def _():
-                pltpu.make_async_remote_copy(
-                    src_ref=source,
-                    dst_ref=recv.at[me],
-                    send_sem=send.at[i],
-                    recv_sem=pr_sem.at[me],
-                    device_id=(enc, owner),
-                    device_id_type=MESH,
-                ).start()
-
-            @pl.when(me == owner)
+                piece_copy(source, side_of, i, send).start()
+
+            @pl.when(me == 2 * i + side_of)
             def _():
-                recv[me] = source[...]
-
-    def sent_pieces(side, send, slot):
-        for i in range(8):
-            owner = 2 * i + side
-            source = spread.at[
-                slot,
-                pl.ds((i % 4) * group_rows, group_rows),
-                pl.ds((i // 4) * half_feats, half_feats),
-            ]
-
-            @pl.when(me != owner)
+                recv[slot_of(me)] = piece_of(source, i)[...]
+
+    def sent_pieces(source, side_of, send):
+        for i in range(n // 2):
+
+            @pl.when(me != 2 * i + side_of)
             def _():
-                pltpu.make_async_remote_copy(
-                    src_ref=source,
-                    dst_ref=recv.at[me],
-                    send_sem=send.at[i],
-                    recv_sem=pr_sem.at[me],
-                    device_id=(enc, owner),
-                    device_id_type=MESH,
-                ).wait_send()
-
-    spread[0] = nn(p_low[...], x[...]).astype(BF)
-    send_pieces(1, vs_sem, 0)
-
-    def q_step(j):
-        cols = chunk(j, 256)
-        y = nn(x[...], w_qkv[:, cols]) + q_bias[:, cols]
-        q[:, cols] = (y.astype(BF).astype(F32) * head_scale).astype(BF)
-
-    loop(width // 256, q_step)
+                piece_copy(source, side_of, i, send).wait_send()
+
+    px[...] = nn(p_low[...], x[...]).astype(BF)
+    send_pieces(px, 1, vs_sem)
+
+    y = nn(x[...], w_qkv[:, query_w]) + q_bias[...]
+    q[...] = (y.astype(BF).astype(F32) * head_scale).astype(BF)
 
     def attend_row(r):
         place0 = iota((length, 1), 0)
@@ -635,19 +676,19 @@
         count0 = jnp.zeros((length, 1), jnp.int32)
         count1 = jnp.zeros((1, length), jnp.int32)
         for k in range(DOCS):
-            start = starts[r * DOCS + k]
+            start = starts[0, r, k]
             count0 = count0 + (place0 >= start).astype(jnp.int32)
             count1 = count1 + (place1 >= start).astype(jnp.int32)
         seg_bias[...] = jnp.where(count0 == count1, 0.0, NEG)
-        these = chunk(r, length)
+        these = pl.ds(r * length, length)
         mask_even = jnp.where(low_half, 1.0, 0.0).astype(BF)
         mask_odd = jnp.where(low_half, 0.0, 1.0).astype(BF)
 
-        def attend_pair(p):
-            lanes = chunk(p, 128)
+        for p in range(pairs):
+            lanes = pl.ds(p * 128, 128)
             query = q[these, lanes]
             key = kv[these, lanes]
-            value = kv[these, pl.ds(pl.multiple_of(width + p * 128, 128), 128)]
+            value = kv[these, pl.ds(width + p * 128, 128)]
             ext = jnp.concatenate([value, jnp.ones_like(value)], axis=1)
             outs = []
             for mask in (mask_even, mask_odd):
@@ -659,31 +700,16 @@
             low = jnp.where(low_half, even[:, 128:], odd[:, 128:])
             mix[these, lanes] = (top / low).astype(BF)
 
-        loop(pairs, attend_pair)
-
-    loop(rows, attend_row)
-
-    def saver(source, target, index):
-        return pltpu.make_async_copy(source, target, save_sem.at[index])
-
-    saves = []
-
-    def save(source, target, index):
-        copy = saver(source, target, index)
-        copy.start()
-        saves.append(copy)
-
-    shared(xcls.at[own_rows], rows_of(xcls), xs_sem, xr_sem)
-    save(xcls, xcls_o, 0)
-    shared(mixed.at[own_rows], rows_of(mixed), ms_sem, mr_sem)
-    save(mixed, mixed_o, 1)
-    loads[3].wait()
-
-    def out_step(j):
-        cols = chunk(j, 256)
-        acc[:, cols] = nn(mixed[...], w_out[:, cols]) + o_bias[:, cols] + xcls[:, cols].astype(F32)
-
-    loop(width // 256, out_step)
+    attend_row(0)
+
+    shared(xcls.at[core, own], xcls_place, xs_sem, xr_sem)
+    xcls_over = remote(xcls.at[core], xcls.at[core], fs_sem.at[10], fr_sem.at[10], (enc, sibling))
+    xcls_over.start()
+    xcls_back = remote(xcls.at[core], xcls.at[1 - core], fs_sem.at[10], fr_sem.at[10], (enc, sibling))
+    shared(mixed.at[own], mixed_place, ms_sem, mr_sem)
+    loads[4].wait()
+
+    acc[...] = nn(mixed[...], w_out[...]) + o_bias[...] + xcls[core].astype(F32)
 
     def stats(h):
         centred = h - jnp.mean(h, -1, keepdims=True)
@@ -694,144 +720,97 @@
     norm1[...] = unit
     inv1[...] = jnp.broadcast_to(inverse, inv1.shape)
     level = unit * gain1[...] + shift1[...]
-    normed[...] = level
-    low_t[...] = level.astype(BF)
-    loads[4].wait()
+    normed[...] = level.astype(BF)
     loads[5].wait()
-    acc[...] = level + d_bias[...]
-
-    def ff_step(j):
-        cols = chunk(j, 512)
-        inner = nn(low_t[...], w_up[:, cols]) + u_bias[:, cols]
-        cdf, pdf = gelu_parts(inner)
-        slope[:, cols] = cdf + inner * pdf
-        active = (inner * cdf).astype(BF)
-        act[:, cols] = active
-        acc[...] += nn(active, w_down[cols, :])
-
-    loop(ff // 512, ff_step)
-    normed_keep = saver(low_t, normed_o, 2)
-    normed_keep.start()
-    save(act, act_o, 3)
-    unit, inverse = stats(acc[...])
+    loads[6].wait()
+    inner = nn(normed[...], w_up[...]) + u_bias[...]
+    cdf, pdf = gelu_parts(inner)
+    slope[...] = cdf + inner * pdf
+    act[...] = (inner * cdf).astype(BF)
+    unit, inverse = stats(level + d_bias[...] + nn(act[...], w_down[...]))
     norm2[...] = unit
     inv2[...] = jnp.broadcast_to(inverse, inv2.shape)
-    cls[enc] = (unit * gain2[...] + shift2[...]).astype(BF)
-    half = wide // 2
-    mine = pl.ds(pl.multiple_of(core * half, half), half)
-    theirs = pl.ds(pl.multiple_of((1 - core) * half, half), half)
-    cross = pltpu.make_async_remote_copy(
-        src_ref=cls.at[enc, mine],
-        dst_ref=cls.at[enc, mine],
-        send_sem=cs_sem.at[0],
-        recv_sem=cr_sem.at[0],
-        device_id=(other, me),
-        device_id_type=MESH,
-    )
-    cross.start()
-    cross_in = pltpu.make_async_remote_copy(
-        src_ref=cls.at[enc, mine],
-        dst_ref=cls.at[other, mine],
-        send_sem=cs_sem.at[0],
-        recv_sem=cr_sem.at[0],
-        device_id=(other, me),
-        device_id_type=MESH,
-    )
-    pass_on = pltpu.make_async_remote_copy(
-        src_ref=cls.at[other, mine],
-        dst_ref=cls.at[other, mine],
-        send_sem=cs_sem.at[1],
-        recv_sem=cr_sem.at[1],
-        device_id=(enc, sibling),
-        device_id_type=MESH,
-    )
-    pass_in = pltpu.make_async_remote_copy(
-        src_ref=cls.at[other, mine],
-        dst_ref=cls.at[other, theirs],
-        send_sem=cs_sem.at[1],
-        recv_sem=cr_sem.at[1],
-        device_id=(enc, sibling),
-        device_id_type=MESH,
-    )
-
-    place_row = iota((1, wide), 1)
+    cls[enc, core] = (unit * gain2[...] + shift2[...]).astype(BF)
+
+    def cls_copy(half_of, to_core, index, device):
+        return remote(
+            cls.at[half_of, core], cls.at[half_of, to_core], cs_sem.at[index], cr_sem.at[index], device
+        )
+
+    cls_copy(enc, core, 0, (other, me)).start()
+    cls_copy(enc, core, 1, (enc, sibling)).start()
+    give(mixed, mixed_o, 1)
+    give(normed, normed_o, 2)
+    give(act, act_o, 3)
+
+    def padded(question):
+        device = lax.div(question, local)
+        place = lax.rem(device, 2) * side + lax.div(device, 2) * PAD
+        return place + question - device * local
+
+    place_row = iota((1, 2 * side), 1)
 
     def place_step(device, row):
         for k in range(local):
-            target = positives[device * local + k]
-            padded = target + (PAD - local) * lax.div(target, local)
-            row = jnp.where(place_row == device * PAD + k, padded, row)
+            question = device * local + k
+            row = jnp.where(place_row == padded(question), padded(positives[question]), row)
         return row
 
-    pos_row = lax.fori_loop(0, n, place_step, jnp.full((1, wide), -1, jnp.int32))
+    pos_row = lax.fori_loop(0, n, place_step, jnp.full((1, 2 * side), -1, jnp.int32))
+
+    xcls_back.wait_recv()
 
     @pl.when(core == 0)
     def _():
-        for j in range(width // 256):
-            cols = pl.ds(j * 256, 256)
-            y = (nn(xcls[...], w_qkv[:, cols]) + q_bias[:, cols]).astype(BF).astype(F32)
-            turned[pl.ds(j * 256, 256), :] = y.T.astype(BF)
-
-    normed_keep.wait()
-
-    def layer_tile(r):
-        these = chunk(r, length)
-
-        def tile_out(j):
-            cols = chunk(j, 256)
-            y = nn(mix[these, :], w_out[:, cols]) + o_bias[:, cols]
-            acc_t[:, cols] = y + x[these, cols].astype(F32)
-
-        loop(width // 256, tile_out)
-        unit, _ = stats(acc_t[...])
-        level = unit * gain1[...] + shift1[...]
-        normed_t[...] = level
-        low_t[...] = level.astype(BF)
-        acc_t[...] = level + d_bias[...]
-
-        def tile_ff(j):
-            cols = chunk(j, 512)
-            inner = nn(low_t[...], w_up[:, cols]) + u_bias[:, cols]
-            active = 0.5 * inner * (1.0 + lax.erf(inner * ROOT_HALF))
-            acc_t[...] += nn(active.astype(BF), w_down[cols, :])
-
-        loop(ff // 512, tile_ff)
-        unit, _ = stats(acc_t[...])
-        hout[these, :] = (unit * gain2[...] + shift2[...]).astype(BF)
-
-    def save_tile(r):
-        these = pl.ds(r * length, length)
-        save(hout.at[these], hidden_out.at[these], 8 + r)
-
-    layer_tile(0)
-    save_tile(0)
-
-    cross.wait_send()
-    cross_in.wait_recv()
-    pass_on.start()
-    pass_on.wait_send()
-    pass_in.wait_recv()
+        for c in range(2):
+            y = (nn(xcls[c], w_qkv[:, query_w]) + q_bias[...]).astype(BF).astype(F32)
+            turned[:, pl.ds(c * side, side)] = y.T.astype(BF)
+
+    save(xcls.at[0], xcls_o.at[pl.ds(0, side)], 4)
+    save(xcls.at[1], xcls_o.at[pl.ds(side, side)], 5)
+
+    attend_row(1)
+    attend_row(2)
+
+    cls_copy(enc, core, 0, (other, me)).wait_send()
+    cls_in = remote(cls.at[enc, core], cls.at[other, core], cs_sem.at[0], cr_sem.at[0], (other, me))
+    cls_in.wait_recv()
+    cls_pass = cls_copy(other, core, 2, (enc, sibling))
+    cls_pass.start()
+    cls_copy(enc, core, 1, (enc, sibling)).wait_send()
+    remote(
+        cls.at[enc, core], cls.at[enc, 1 - core], cs_sem.at[1], cr_sem.at[1], (enc, sibling)
+    ).wait_recv()
+    cls_pass.wait_send()
+    remote(
+        cls.at[other, core], cls.at[other, 1 - core], cs_sem.at[2], cr_sem.at[2], (enc, sibling)
+    ).wait_recv()
 
     sim_scale = width ** (-0.5)
-    good_col = lax.rem(iota((wide, 1), 0), PAD) < local
-    good_row = lax.rem(iota((1, wide), 1), PAD) < local
-    raw_sims = sim_scale * nt(cls[1], cls[0])
+    good_col = lax.rem(iota((2 * side, 1), 0), PAD) < local
+    good_row = lax.rem(iota((1, 2 * side), 1), PAD) < local
+    questions = cls[0].reshape(2 * side, width)
+    passages = cls[1].reshape(2 * side, width)
+    raw_sims = sim_scale * nt(passages, questions)
     sims = jnp.where(good_col, raw_sims, NEG)
     sim_peak = jnp.max(sims, 0, keepdims=True)
     sim_total = sim_peak + jnp.log(jnp.sum(jnp.exp(sims - sim_peak), 0, keepdims=True))
-    target = (iota((wide, wide), 0) == pos_row).astype(F32)
+    target = (iota((2 * side, 2 * side), 0) == pos_row).astype(F32)
     losses = sim_total - jnp.sum(raw_sims * target, 0, keepdims=True)
     loss = jnp.sum(jnp.where(good_row, losses, 0.0), -1, keepdims=True) / (local * n)
     d_sims = sim_scale * (jnp.exp(sims - sim_total) - target) / local
     d_sims = jnp.where(good_row, d_sims, 0.0).astype(BF)
 
-    @pl.when(enc == 0)
-    def _():
-        d_cls[...] = tn(d_sims, cls[1])
-
-    @pl.when(enc == 1)
-    def _():
-        d_cls[...] = nn(d_sims, cls[0])
+    for c in range(2):
+        these = slice(c * side, (c + 1) * side)
+
+        @pl.when((enc == 0) & (core == c))
+        def _():
+            d_cls[...] = tn(d_sims[:, these], passages)
+
+        @pl.when((enc == 1) & (core == c))
+        def _():
+            d_cls[...] = nn(d_sims[these, :], questions)
 
     def column_sum(value):
         return jnp.sum(value, 0, keepdims=True)
@@ -847,49 +826,62 @@
     vecs[pl.ds(0, 1), :] = column_sum(d_cls[...] * norm2[...])
     vecs[pl.ds(1, 1), :] = column_sum(d_cls[...])
     d_second = back(d_cls[...], norm2[...], inv2[...], gain2[...])
-    acc[...] = d_second
-    d_outer = d_second.astype(BF)
-    douter[...] = d_outer
-    save(douter, douter_o, 4)
-    vecs[pl.ds(2, 1), :] = column_sum(d_outer.astype(F32))
-
-    def ff_back(j):
-        cols = chunk(j, 512)
-        d_active = nt(douter[...], w_down[cols, :])
-        d_low = (d_active * slope[:, cols]).astype(BF)
-        dinner[:, cols] = d_low
-        up_sum[:, cols] = column_sum(d_low.astype(F32))
-        acc[...] += nt(d_low, w_up[:, cols])
-
-    loop(ff // 512, ff_back)
-    save(dinner, dinner_o, 5)
-    vecs[pl.ds(3, 1), :] = column_sum(acc[...] * norm1[...])
-    vecs[pl.ds(4, 1), :] = column_sum(acc[...])
+    douter[...] = d_second.astype(BF)
+    d_active = nt(douter[...], w_down[...])
+    dinner[...] = (d_active * slope[...]).astype(BF)
+    acc[...] = d_second + nt(dinner[...], w_up[...])
+    vecs[pl.ds(2, 1), :] = column_sum(acc[...] * norm1[...])
+    vecs[pl.ds(3, 1), :] = column_sum(acc[...])
+    vecs[pl.ds(4, 1), :] = jnp.broadcast_to(loss, (1, width))
+    vecs[pl.ds(6, 2), :] = jnp.zeros((2, width), F32)
     d_first = back(acc[...], norm1[...], inv1[...], gain1[...])
     dfirst[...] = d_first
-    d_low = d_first.astype(BF)
-    datt[...] = d_low
-    save(datt, datt_o, 6)
-    vecs[pl.ds(5, 1), :] = column_sum(d_low.astype(F32))
-
-    def mix_back(j):
-        cols = chunk(j, 256)
-        dmix[:, cols] = nt(datt[...], w_out[cols, :]).astype(BF)
-
-    loop(width // 256, mix_back)
-    vecs[pl.ds(6, 1), :] = column_sum(dmix[...].astype(F32))
-    vecs[pl.ds(7, 1), :] = jnp.broadcast_to(loss, (1, width))
-
-    which = lax.div(me, 2)
+    datt[...] = d_first.astype(BF)
+
+    dmix[core] = nt(datt[...], w_out[...]).astype(BF)
+    dmix_over = remote(dmix.at[core], dmix.at[core], fs_sem.at[11], fr_sem.at[11], (enc, sibling))
+    dmix_back = remote(dmix.at[core], dmix.at[1 - core], fs_sem.at[11], fr_sem.at[11], (enc, sibling))
+
+    @pl.when(core == 0)
+    def _():
+        dmix_over.start()
+
+    block_diagonal(dbd, dmix[core, own, :].astype(F32))
+    d_weights = nt(dbd[...], kv[:, pl.ds(width, width)])
+    weights = probs[...]
+    inner_sum = jnp.sum(d_weights * weights, -1, keepdims=True)
+    ds_low[...] = (head_scale * weights * (d_weights - inner_sum)).astype(BF)
+    dx[...] = nn(ds_low[...], x[...]).astype(BF)
+    send_pieces(dx, 0, ks_sem)
+    dq_own[...] = own_lanes(nn(ds_low[...], kv[:, pl.ds(0, width)])).astype(BF)
+
+    def dq_place(peer):
+        return dq_o.at[block(slot_of(peer))]
+
+    queries = Relay(dq_own, dq_place, qs_sem, qr_sem)
+    queries.start()
+    save(dq_own, dq_place(me), 6)
+    give(douter, douter_o, 7)
+    give(dinner, dinner_o, 8)
+    give(datt, datt_o, 9)
+    vecs[pl.ds(5, 1), :] = column_sum(dmix[core].astype(F32))
+
+    def layer_tile(r):
+        these = pl.ds(r * length, length)
+
+        acc_t[...] = nn(mix[these, :], w_out[...]) + o_bias[...] + x[these, :].astype(F32)
+        unit, _ = stats(acc_t[...])
+        level = unit * gain1[...] + shift1[...]
+        low_t[...] = level.astype(BF)
+        inner = nn(low_t[...], w_up[...]) + u_bias[...]
+        active = (0.5 * inner * (1.0 + lax.erf(inner * ROOT_HALF))).astype(BF)
+        unit, _ = stats(level + d_bias[...] + nn(active, w_down[...]))
+        hout[these, :] = (unit * gain2[...] + shift2[...]).astype(BF)
+        save(hout.at[these], hidden_out.at[these], 13 + r)
+
     group = lax.rem(which, 4)
 
-    planes = n // 4
-    across = me + 2 - 4 * lax.rem(which, 2)
-
-    def up_down(j):
-        return lax.rem(me + 4 * j + 4, n)
-
-    def grad_of(peer):
+    def grad_place(peer):
         index = lax.div(peer, 2)
         return kv_o.at[
             lax.rem(peer, 2),
@@ -897,105 +889,71 @@
             pl.ds(pl.multiple_of(lax.div(index, 4) * half_feats, half_feats), half_feats),
         ]
 
-    def gradient(slot, source, owner, device):
-        return remote(source, grad_of(owner), gs_sem.at[slot], gr_sem.at[owner], (enc, device))
+    summed = Relay(piece, grad_place, gs_sem, gr_sem)
+    piece_save = pltpu.make_async_copy(piece, grad_place(me), save_sem.at[16])
 
     def sum_pieces():
-        def wait(j):
+        def came(j):
             peer = lax.rem(me + j + 1, n)
-            pltpu.make_async_remote_copy(
-                src_ref=recv.at[peer],
-                dst_ref=recv.at[peer],
-                send_sem=vs_sem.at[0],
-                recv_sem=pr_sem.at[peer],
-                device_id=(enc, peer),
-                device_id_type=MESH,
-            ).wait_recv()
-
-        loop(n - 1, wait)
+            place = recv.at[slot_of(peer)]
+            remote(place, place, ks_sem.at[0], kr_sem.at[peer], (enc, peer)).wait_recv()
+
+        loop(n - 1, came)
         for a in range(H // 4):
-            right = recv[:, pl.ds(a * PAD, PAD), :].reshape(wide, half_feats)
+            right = recv[:, pl.ds(a * PAD, PAD), :].reshape(2 * side, half_feats)
             left = turned[pl.ds(pl.multiple_of(group * group_cols + a * head, head), head), :]
             piece[pl.ds(a * head, head), :] = nn(left, right).astype(BF)
-        for j in range(planes - 1):
-            gradient(j, piece, me, up_down(j)).start()
-        gradient(planes - 1, piece, me, across).start()
-        gradient(planes, piece, me, sibling).start()
-        saver(piece, grad_of(me), 7).start()
-
-    def pass_plane():
-        for j in range(planes - 1):
-            peer = up_down(j)
-            gradient(0, grad_of(peer), peer, peer).wait_recv()
-            gradient(planes + 1 + 2 * j, grad_of(peer), peer, across).start()
-            gradient(planes + 2 + 2 * j, grad_of(peer), peer, sibling).start()
-
-    def pass_across():
-        for j in range(planes):
-            peer = across if j == 0 else lax.rem(up_down(j - 1) - me + across + n, n)
-            gradient(0, grad_of(peer), peer, across).wait_recv()
-            gradient(3 * planes - 1 + j, grad_of(peer), peer, sibling).start()
-
-    def finish_gradients():
-        def came(j):
-            peer = lax.rem(same_core(j) + 1 - 2 * core + n, n)
-            gradient(0, grad_of(peer), peer, sibling).wait_recv()
-
-        loop(n // 2, came)
-
-        def sent(j):
-            remote(piece, grad_of(me), gs_sem.at[j], gr_sem.at[me], (enc, sibling)).wait_send()
-
-        loop(4 * planes - 1, sent)
-        saver(piece, grad_of(me), 7).wait()
+        summed.start()
+        piece_save.start()
 
     @pl.when(core == 1)
     def _():
-        for j in range(width // 256):
-            cols = pl.ds(j * 256, 256)
-            turned[pl.ds(j * 256, 256), :] = dmix[:, cols].astype(F32).T.astype(BF)
+        dmix_back.wait_recv()
+        for c in range(2):
+            turned[:, pl.ds(c * side, side)] = dmix[c].astype(F32).T.astype(BF)
         sum_pieces()
 
-    d_own = dmix[own_rows, :].astype(F32)
-    block_diagonal(dbd, d_own)
-    d_weights = nt(dbd[...], kv[:, pl.ds(width, width)])
-    weights = probs[...]
-    inner_sum = jnp.sum(d_weights * weights, -1, keepdims=True)
-    ds_low[...] = (head_scale * weights * (d_weights - inner_sum)).astype(BF)
-    spread[1] = nn(ds_low[...], x[...]).astype(BF)
-    send_pieces(0, ks_sem, 1)
-    d_query = own_lanes(nn(ds_low[...], kv[:, pl.ds(0, width)])).astype(BF)
-    dq_own[...] = d_query
-    share(dq_own, rows_of(dq_o), qs_sem, qr_sem)
-    save(dq_own, dq_o.at[own_rows], 11)
-
+    layer_tile(0)
     layer_tile(1)
-    save_tile(1)
+    queries.plane()
 
     @pl.when(core == 0)
     def _():
         sum_pieces()
 
     layer_tile(2)
-    save_tile(2)
-
-    spread_q = nt(qbd[...], w_qkv[:, pl.ds(width, width)]).astype(BF)
-    spread_v = nt(dbd[...], w_qkv[:, pl.ds(2 * width, width)]).astype(BF)
-    base = dfirst[own_rows, :] + nt(dq_own[...], w_qkv[:, pl.ds(0, width)])
+    queries.over()
+    summed.plane()
+
+    base = dfirst[own, :] + nt(dq_own[...], w_qkv[:, query_w])
     base = base.astype(BF)
-    for r in range(rows):
-        these = slice(r * length, (r + 1) * length)
-        y = tn(ds_low[:, these], spread_q) + tn(p_low[:, these], spread_v) + tn(pick[:, these], base)
-        hgrad[pl.ds(r * length, length), :] = y.astype(BF)
-    save(hgrad, hidden_grad, 12)
-
-    sent_pieces(1, vs_sem, 0)
-    sent_pieces(0, ks_sem, 1)
-    shared(dq_own, rows_of(dq_o), qs_sem, qr_sem)
-
-    pass_plane()
-    pass_across()
-    finish_gradients()
+    qk[...] = nt(qbd[...], w_qkv[:, key_w]).astype(BF)
+    dv[...] = nt(dbd[...], w_qkv[:, value_w]).astype(BF)
+    y = tn(ds_low[...], qk[...]) + tn(p_low[...], dv[...]) + tn(pick, base)
+    hgrad[...] = y.astype(BF)
+    save(hgrad, hidden_grad, 17)
+    vecs_give = remote(vecs, vecs_o.at[core], fs_sem.at[12], fr_sem.at[12], (enc, sibling))
+    vecs_give.start()
+    vecs_take = remote(vecs, vecs_o.at[1 - core], fs_sem.at[12], fr_sem.at[12], (enc, sibling))
+    save(vecs, vecs_o.at[core], 12)
+
+    summed.over()
+    sent_pieces(px, 1, vs_sem)
+    sent_pieces(dx, 0, ks_sem)
+    queries.sent()
+    queries.came()
+    xcls_back.wait_send()
+
+    @pl.when(core == 0)
+    def _():
+        dmix_over.wait_send()
+
+    for copy in [*given, vecs_take]:
+        copy.wait_send()
+        copy.wait_recv()
+    summed.sent()
+    piece_save.wait()
+    summed.came()
     for copy in saves:
         copy.wait()
 
@@ -1013,7 +971,6 @@
     hidden_out_i,
     hidden_grad_i,
     vecs,
-    up_sum,
     loss,
     hidden_out,
     hidden_grad,
@@ -1049,85 +1006,76 @@
     out_sem,
 ):
     width = xcls.shape[1]
-    ff = act.shape[1]
-    pairs = [
-        (act_i, act),
-        (douter_i, douter),
-        (normed_i, normed),
-        (dinner_i, dinner),
-        (mixed_i, mixed),
-        (datt_i, datt),
-        (xcls_i, xcls),
-        (dq_i, dq),
-        (kv_i, kv),
+    ins = {}
+    loads = [
+        ("mixed", mixed_i, mixed),
+        ("datt", datt_i, datt),
+        ("act", act_i, act),
+        ("douter", douter_i, douter),
+        ("normed", normed_i, normed),
+        ("dinner", dinner_i, dinner),
+        ("xcls", xcls_i, xcls),
+        ("dq", dq_i, dq),
+        ("kv", kv_i, kv),
+        ("h_out", hidden_out_i, h_out),
+        ("h_grad", hidden_grad_i, h_grad),
     ]
-    ins = [pltpu.make_async_copy(a, b, in_sem.at[i]) for i, (a, b) in enumerate(pairs)]
-    for copy in ins:
-        copy.start()
-    through_in = [
-        pltpu.make_async_copy(hidden_out_i, h_out, in_sem.at[9]),
-        pltpu.make_async_copy(hidden_grad_i, h_grad, in_sem.at[10]),
-    ]
-    for copy in through_in:
-        copy.start()
-
-    loss[...] = vecs[pl.ds(7, 1), pl.ds(0, 1)]
-    grad_second_gain[...] = vecs[pl.ds(0, 1), :]
-    grad_second_shift[...] = vecs[pl.ds(1, 1), :]
-    grad_down_bias[...] = vecs[pl.ds(2, 1), :]
-    grad_first_gain[...] = vecs[pl.ds(3, 1), :]
-    grad_first_shift[...] = vecs[pl.ds(4, 1), :]
-    grad_out_bias[...] = vecs[pl.ds(5, 1), :]
-    grad_value_bias[...] = vecs[pl.ds(6, 1), :]
-    grad_up_bias[...] = up_sum[...]
-
-    ins[0].wait()
-    ins[1].wait()
-
-    def down_step(j):
-        these = chunk(j, 256)
+    for index, (name, source, target) in enumerate(loads):
+        ins[name] = pltpu.make_async_copy(source, target, in_sem.at[index])
+        ins[name].start()
+
+    def column_sum(value):
+        return jnp.sum(value.astype(F32), 0, keepdims=True)
+
+    def vector(row):
+        return vecs[0, pl.ds(row, 1), :] + vecs[1, pl.ds(row, 1), :]
+
+    def put(source, target, rows, index):
+        pltpu.make_async_copy(source.at[rows], target.at[0, rows], out_sem.at[index]).start()
+
+    loss[...] = vecs[0, pl.ds(4, 1), pl.ds(0, 1)]
+    grad_second_gain[...] = vector(0)
+    grad_second_shift[...] = vector(1)
+    grad_first_gain[...] = vector(2)
+    grad_first_shift[...] = vector(3)
+    grad_value_bias[...] = vector(5)
+
+    ins["mixed"].wait()
+    ins["datt"].wait()
+    g_out[...] = tn(mixed[...], datt[...])
+    put(g_out, grad_out, pl.ds(0, width), 4)
+    ins["act"].wait()
+    ins["douter"].wait()
+    for j in range(4):
+        these = pl.ds(j * width, width)
         g_down[these, :] = tn(act[:, these], douter[...])
-        pltpu.make_async_copy(g_down.at[these], grad_down.at[0, these], out_sem.at[2]).start()
-
-    loop(ff // 256, down_step)
-    ins[2].wait()
-    ins[3].wait()
-
-    def up_step(j):
-        these = chunk(j, 128)
+        put(g_down, grad_down, these, 2)
+    ins["normed"].wait()
+    ins["dinner"].wait()
+    for j in range(3):
+        these = pl.ds(j * 256, 256)
         g_up[these, :] = tn(normed[:, these], dinner[...])
-        pltpu.make_async_copy(g_up.at[these], grad_up.at[0, these], out_sem.at[3]).start()
-
-    loop(width // 128, up_step)
+        put(g_up, grad_up, these, 3)
+    ins["xcls"].wait()
+    ins["dq"].wait()
+    ins["kv"].wait()
+    for j in range(3):
+        these = pl.ds(j * 256, 256)
+        g_qkv[these, pl.ds(0, width)] = tn(xcls[:, these], dq[...])
+        for m in range(2):
+            g_qkv[these, pl.ds((m + 1) * width, width)] = kv[m, :, these].astype(F32).T
+        put(g_qkv, grad_qkv, these, 5)
     through = [
         pltpu.make_async_copy(h_out, hidden_out, out_sem.at[0]),
         pltpu.make_async_copy(h_grad, hidden_grad, out_sem.at[1]),
     ]
-    for came, copy in zip(through_in, through):
-        came.wait()
+    for name, copy in zip(("h_out", "h_grad"), through):
+        ins[name].wait()
         copy.start()
-    ins[4].wait()
-    ins[5].wait()
-
-    def out_step(j):
-        these = chunk(j, 128)
-        g_out[these, :] = tn(mixed[:, these], datt[...])
-        pltpu.make_async_copy(g_out.at[these], grad_out.at[0, these], out_sem.at[4]).start()
-
-    loop(width // 128, out_step)
-    ins[6].wait()
-    ins[7].wait()
-    ins[8].wait()
-    grad_query_bias[...] = jnp.sum(dq[...].astype(F32), 0, keepdims=True)
-
-    def qkv_step(j):
-        these = chunk(j, 128)
-        g_qkv[these, pl.ds(0, width)] = tn(xcls[:, these], dq[...])
-        for m in range(2):
-            g_qkv[these, pl.ds((m + 1) * width, width)] = kv[m, :, these].astype(F32).T
-        pltpu.make_async_copy(g_qkv.at[these], grad_qkv.at[0, these], out_sem.at[5]).start()
-
-    loop(width // 128, qkv_step)
+    grad_down_bias[...] = column_sum(douter[...])
+    grad_up_bias[...] = column_sum(dinner[...])
+    grad_out_bias[...] = column_sum(datt[...])
+    grad_query_bias[...] = column_sum(dq[...])
     pltpu.make_async_copy(g_down, grad_down.at[0], out_sem.at[2]).wait()
     pltpu.make_async_copy(g_up, grad_up.at[0], out_sem.at[3]).wait()
     pltpu.make_async_copy(g_out, grad_out.at[0], out_sem.at[4]).wait()
@@ -1159,7 +1107,9 @@
     tokens = rows * length
     ff = up_weight.shape[-1]
     wide = n * PAD
+    side = wide // 2
     spreads = H * PAD
+    planes = n // 4
     shape = jax.ShapeDtypeStruct
     hbm = pl.BlockSpec(memory_space=pl.ANY)
     vmem = pl.BlockSpec(memory_space=pltpu.VMEM)
@@ -1179,12 +1129,11 @@
             shape((wide, ff), BF),
             shape((wide, width), BF),
             shape((wide, width), BF),
+            shape((2, 8, width), F32),
             shape((2, width, width), BF),
-            shape((8, width), F32),
-            shape((1, ff), F32),
         ],
         in_specs=[smem, smem, hbm, hbm, vmem, vmem, hbm, vmem, vmem, vmem, hbm, vmem, hbm, vmem, vmem, vmem],
-        out_specs=[hbm] * 11 + [vmem] * 2,
+        out_specs=[hbm] * 12,
         scratch_shapes=[
             pltpu.VMEM((tokens, width), BF),
             pltpu.VMEM((width, 3 * width), BF),
@@ -1197,58 +1146,63 @@
             pltpu.VMEM((length, length), F32),
             pltpu.VMEM((spreads, width), BF),
             pltpu.VMEM((spreads, width), BF),
+            pltpu.VMEM((spreads, width), BF),
+            pltpu.VMEM((spreads, width), BF),
             pltpu.VMEM((spreads, tokens), F32),
             pltpu.VMEM((spreads, tokens), BF),
             pltpu.VMEM((spreads, tokens), BF),
-            pltpu.VMEM((2, spreads, width), BF),
-            pltpu.VMEM((wide, width), BF),
-            pltpu.VMEM((wide, width), BF),
-            pltpu.VMEM((2, wide, width), BF),
-            pltpu.VMEM((wide, width), F32),
-            pltpu.VMEM((wide, width), F32),
-            pltpu.VMEM((wide, 128), F32),
-            pltpu.VMEM((wide, width), F32),
-            pltpu.VMEM((wide, 128), F32),
-            pltpu.VMEM((wide, ff), BF),
-            pltpu.VMEM((wide, ff), F32),
-            pltpu.VMEM((wide, ff), BF),
-            pltpu.VMEM((wide, width), BF),
-            pltpu.VMEM((wide, width), BF),
-            pltpu.VMEM((wide, width), BF),
-            pltpu.VMEM((wide, width), F32),
-            pltpu.VMEM((wide, width), F32),
-            pltpu.VMEM((wide, width), F32),
+            pltpu.VMEM((spreads, width), BF),
+            pltpu.VMEM((spreads, width), BF),
+            pltpu.VMEM((2, side, width), BF),
+            pltpu.VMEM((side, width), BF),
+            pltpu.VMEM((2, 2, side, width), BF),
+            pltpu.VMEM((side, width), F32),
+            pltpu.VMEM((side, 128), F32),
+            pltpu.VMEM((side, width), F32),
+            pltpu.VMEM((side, 128), F32),
+            pltpu.VMEM((side, width), BF),
+            pltpu.VMEM((side, ff), BF),
+            pltpu.VMEM((side, ff), F32),
+            pltpu.VMEM((side, ff), BF),
+            pltpu.VMEM((side, width), BF),
+            pltpu.VMEM((side, width), BF),
+            pltpu.VMEM((2, side, width), BF),
+            pltpu.VMEM((side, width), F32),
+            pltpu.VMEM((side, width), F32),
+            pltpu.VMEM((side, width), F32),
+            pltpu.VMEM((8, width), F32),
             pltpu.VMEM((width, wide), BF),
             pltpu.VMEM((n, H // 4 * PAD, width // 2), BF),
             pltpu.VMEM((width // 4, width // 2), BF),
             pltpu.VMEM((PAD, width), BF),
-            pltpu.VMEM((length, width), F32),
             pltpu.VMEM((length, width), BF),
             pltpu.VMEM((length, width), F32),
             pltpu.VMEM((tokens, width), BF),
             pltpu.VMEM((tokens, width), BF),
-            dma((6,)),
+            dma((7,)),
+            dma((18,)),
+            dma((n // 2,)),
+            dma((n,)),
+            dma((n // 2,)),
+            dma((n,)),
+            dma((n // 2,)),
+            dma((n,)),
+            dma((3,)),
+            dma((3,)),
+            dma((4 * planes,)),
+            dma((n,)),
+            dma((n // 2,)),
+            dma((4 * planes,)),
+            dma((n,)),
             dma((13,)),
-            dma((n,)),
-            dma((n,)),
-            dma((n,)),
-            dma((n,)),
-            dma((8,)),
-            dma((8,)),
-            dma((n,)),
-            dma((2,)),
-            dma((2,)),
-            dma((n,)),
-            dma((n,)),
-            dma((n,)),
-            dma((n,)),
+            dma((13,)),
         ],
         compiler_params=pltpu.CompilerParams(
             collective_id=0, has_side_effects=True, vmem_limit_bytes=limit
         ),
         name="layer",
     )(
-        starts.reshape(rows * DOCS),
+        starts,
         positives,
         hidden_in.reshape(tokens, width),
         qkv_weight.reshape(width, 3 * width),
@@ -1265,7 +1219,7 @@
         second_gain,
         second_shift,
     )
-    (h_out, h_grad, xcls, mixed, normed, act, douter, dinner, datt, dq, kv, vecs, up_sum) = outs
+    h_out, h_grad, xcls, mixed, normed, act, douter, dinner, datt, dq, vecs, kv = outs
     row = shape((1, width), F32)
     grads = pl.pallas_call(
         grad_kernel,
@@ -1287,7 +1241,7 @@
             row,
             row,
         ],
-        in_specs=[hbm] * 11 + [vmem] * 2,
+        in_specs=[hbm] * 11 + [vmem],
         out_specs=[vmem, hbm, hbm, hbm, vmem, vmem, hbm, vmem, vmem, vmem, hbm, vmem, hbm, vmem, vmem, vmem],
         scratch_shapes=[
             pltpu.VMEM((wide, width), BF),
@@ -1310,12 +1264,12 @@
         ],
         compiler_params=pltpu.CompilerParams(vmem_limit_bytes=limit),
         name="gradients",
-    )(xcls, mixed, normed, act, douter, dinner, datt, dq, kv, h_out, h_grad, vecs, up_sum)
-    block = (1, rows, length, width)
+    )(xcls, mixed, normed, act, douter, dinner, datt, dq, kv, h_out, h_grad, vecs)
+    place = (1, rows, length, width)
     return (
         grads[0].reshape(()),
-        grads[1].reshape(block),
-        grads[2].reshape(block),
+        grads[1].reshape(place),
+        grads[2].reshape(place),
         *grads[3:],
     )
 

time: 106 us -> 86.3 us (0.81)
  the two profiles are of different devices: /device:TPU:0 before, /device:TPU:25 now
where the time goes in v3:
time: 86.3 us; the launch traced here: 86.1 us
  Pallas kernels  84 us (97%)
  local copies, waits for them, and re-layouts  1.26 us (1%)
    pallas_call x1, Pallas kernels, fused_on_device(): pl.pallas_call(functools.partial(main_kernel, n), out_shape=[shape((token...  69.8 us
    pallas_call x1, Pallas kernels, fused_on_device(): pl.pallas_call(grad_kernel, out_shape=[shape((1, 1), F32), shape((tokens,...  14.2 us

profile of v3, /device:TPU:25, one launch (start us, length us, event | category | flops | bytes accessed | tf_op | source)
XLA Modules:
  0.0 86.1 jit_solution(16095126618738315082)
XLA Ops:
  0.6 1.3 %copy.32.starts = s32[1,3,4]{2,1,0:T(4,128)} copy(s32[1,3,4]{2,0,1:T(1,128)} %param.17) | data formatting | bytes 96 | tf_op args[1]
  1.9 69.8 %layer.1 = (bf16[768,768]{1,0:T(8,128)(2,1)}, bf16[768,768]{1,0:T(8,128)(2,1)}, bf16[256,768]{1,0:T(8,128)(2,1)}, bf16[256,768]{1,0:T(8,128)(2,1)}, bf16[256,768...) custom-call(s32[1,3,4]{2,1,0:T(4,128)} %copy.32.starts, ...), custom_call_target="tpu_custom_call" | custom-call | tf_op jit(solution)/shard_map/layer/pallas_call | solution.py:1119
  71.7 14.2 %gradients.1 = (f32[1,1]{1,0:T(1,128)}, bf16[768,768]{1,0:T(8,128)(2,1)}, bf16[768,768]{1,0:T(8,128)(2,1)}, f32[1,768,2304]{2,1,0:T(8,128)}, f32[1,768]{1,0:T(1,...) custom-call(bf16[256,768]{1,0:T(8,128)(2,1)} %get-tuple-element.44.x, ...), custom_call_target="tpu_custom_call" | custom-call | tf_op jit(solution)/shard_map/gradients/pallas_call | solution.py:1224

commit v4 on v3

--- a/solution.py
+++ b/solution.py
@@ -390,6 +390,9 @@
     turned,
     recv,
     piece,
+    turned_v,
+    recv_v,
+    piece_v,
     dq_own,
     low_t,
     acc_t,
@@ -408,8 +411,11 @@
     qs_sem,
     qr_sem,
     vs_sem,
+    vr_sem,
     gs_sem,
     gr_sem,
+    hs_sem,
+    hr_sem,
     fs_sem,
     fr_sem,
 ):
@@ -420,11 +426,10 @@
     which = lax.div(me, 2)
     sibling = me + 1 - 2 * core
     across = me + 2 - 4 * lax.rem(which, 2)
-    planes = n // 4
     tokens, width = x.shape
     ff = w_up.shape[1]
     side = n // 2 * PAD
-    rows = starts.shape[1]
+    rows = starts.shape[0]
     length = tokens // rows
     local = rows * DOCS
     head = width // H
@@ -477,9 +482,6 @@
     def cousin(j):
         return lax.rem(same_core(j) + 1 - 2 * core + n, n)
 
-    def up_down(j):
-        return lax.rem(me + 4 * j + 4, n)
-
     def block(index):
         return pl.ds(pl.multiple_of(index * PAD, PAD), PAD)
 
@@ -501,8 +503,14 @@
         loop(n // 2 - 1, came)
 
     class Relay:
-        def __init__(self, source, place, send, receive):
+        def __init__(self, source, place, send, receive, group):
             self.source, self.place, self.send, self.receive = source, place, send, receive
+            self.base = me - lax.rem(me, group)
+            self.group = group
+            self.ups = group // 4 - 1
+
+        def up(self, device, j):
+            return self.base + lax.rem(device - self.base + 4 * j, self.group)
 
         def copy(self, slot, source, owner, device):
             return remote(
@@ -510,36 +518,34 @@
             )
 
         def start(self):
-            for j in range(planes - 1):
-                self.copy(j, self.source, me, up_down(j)).start()
-            self.copy(planes - 1, self.source, me, across).start()
-            self.copy(planes, self.source, me, sibling).start()
+            for j in range(self.ups):
+                self.copy(j, self.source, me, self.up(me, j + 1)).start()
+            self.copy(self.ups, self.source, me, across).start()
+            self.copy(self.ups + 1, self.source, me, sibling).start()
 
         def plane(self):
-            for j in range(planes - 1):
-                peer = up_down(j)
+            for j in range(self.ups):
+                peer = self.up(me, j + 1)
                 self.copy(0, self.place(peer), peer, peer).wait_recv()
-                self.copy(planes + 1 + 2 * j, self.place(peer), peer, across).start()
-                self.copy(planes + 2 + 2 * j, self.place(peer), peer, sibling).start()
+                self.copy(self.ups + 2 + 2 * j, self.place(peer), peer, across).start()
+                self.copy(self.ups + 3 + 2 * j, self.place(peer), peer, sibling).start()
 
         def over(self):
-            for j in range(planes):
-                peer = across if j == 0 else lax.rem(up_down(j - 1) - me + across + n, n)
+            for j in range(self.ups + 1):
+                peer = self.up(across, j)
                 self.copy(0, self.place(peer), peer, across).wait_recv()
-                self.copy(3 * planes - 1 + j, self.place(peer), peer, sibling).start()
+                self.copy(3 * self.ups + 2 + j, self.place(peer), peer, sibling).start()
 
         def sent(self):
             def wait(j):
                 self.copy(j, self.source, me, sibling).wait_send()
 
-            loop(4 * planes - 1, wait)
+            loop(4 * self.ups + 3, wait)
 
         def came(self):
-            def wait(j):
-                peer = cousin(j)
-                self.copy(0, self.place(peer), peer, sibling).wait_recv()
-
-            loop(n // 2, wait)
+            for j in range(self.ups + 1):
+                for peer in (self.up(sibling, j), self.up(across + sibling - me, j)):
+                    self.copy(0, self.place(peer), peer, sibling).wait_recv()
 
     saves = []
 
@@ -568,11 +574,11 @@
         place = iota((1, length), 1)
         count = jnp.zeros((1, length), jnp.int32)
         for k in range(DOCS):
-            start = starts[0, r, k]
+            start = starts[r, 0, k]
             count = count + (place >= start).astype(jnp.int32)
             order = jnp.int32(0)
             for m in range(DOCS):
-                order = order + jnp.where(starts[0, r, m] <= start, 1, 0)
+                order = order + jnp.where(starts[r, 0, m] <= start, 1, 0)
             here = place_col == r * DOCS + k
             first_col = jnp.where(here, r * length + start, first_col)
             seg_col = jnp.where(here, r * 8 + order, seg_col)
@@ -633,50 +639,53 @@
 
     share(mixed.at[own], mixed_place, ms_sem, mr_sem)
 
+    half_n = n // 2
+
     def slot_of(peer):
-        return lax.rem(peer, 2) * (n // 2) + lax.div(peer, 2)
-
-    def piece_of(source, i):
-        return source.at[
-            pl.ds((i % 4) * group_rows, group_rows), pl.ds((i // 4) * half_feats, half_feats)
-        ]
-
-    def piece_copy(source, side_of, i, send):
-        target = recv.at[slot_of(me)]
-        owner = (enc, 2 * i + side_of)
-        return remote(piece_of(source, i), target, send.at[i], kr_sem.at[me], owner)
-
-    def send_pieces(source, side_of, send):
-        for i in range(n // 2):
-
-            @pl.when(me != 2 * i + side_of)
+        return lax.rem(peer, 2) * half_n + lax.div(peer, 2)
+
+    def send_pieces(source, into, owners, send, receive):
+        for j, owner in enumerate(owners):
+            i = j % half_n
+            part = source.at[
+                pl.ds((i % 4) * group_rows, group_rows), pl.ds((i // 4) * half_feats, half_feats)
+            ]
+
+            @pl.when(me != owner)
             def _():
-                piece_copy(source, side_of, i, send).start()
-
-            @pl.when(me == 2 * i + side_of)
+                remote(part, into.at[slot_of(me)], send.at[j], receive.at[me], (enc, owner)).start()
+
+            @pl.when(me == owner)
             def _():
-                recv[slot_of(me)] = piece_of(source, i)[...]
-
-    def sent_pieces(source, side_of, send):
-        for i in range(n // 2):
-
-            @pl.when(me != 2 * i + side_of)
+                into[slot_of(me)] = part[...]
+
+    def sent_pieces(source, into, owners, send, receive):
+        part = source.at[pl.ds(0, group_rows), pl.ds(0, half_feats)]
+        for j, owner in enumerate(owners):
+
+            @pl.when(me != owner)
             def _():
-                piece_copy(source, side_of, i, send).wait_send()
-
+                remote(
+                    part, into.at[slot_of(me)], send.at[j], receive.at[me], (enc, owner)
+                ).wait_send()
+
+    def pieces_came(into, receive):
+        def came(j):
+            peer = lax.rem(me + j + 1, n)
+            place = into.at[slot_of(peer)]
+            remote(place, place, ks_sem.at[0], receive.at[peer], (enc, peer)).wait_recv()
+
+        loop(n - 1, came)
+
+    key_owners = range(0, n, 2)
     px[...] = nn(p_low[...], x[...]).astype(BF)
-    send_pieces(px, 1, vs_sem)
-
-    y = nn(x[...], w_qkv[:, query_w]) + q_bias[...]
-    q[...] = (y.astype(BF).astype(F32) * head_scale).astype(BF)
-
     def attend_row(r):
         place0 = iota((length, 1), 0)
         place1 = iota((1, length), 1)
         count0 = jnp.zeros((length, 1), jnp.int32)
         count1 = jnp.zeros((1, length), jnp.int32)
         for k in range(DOCS):
-            start = starts[0, r, k]
+            start = starts[r, 0, k]
             count0 = count0 + (place0 >= start).astype(jnp.int32)
             count1 = count1 + (place1 >= start).astype(jnp.int32)
         seg_bias[...] = jnp.where(count0 == count1, 0.0, NEG)
@@ -700,13 +709,12 @@
             low = jnp.where(low_half, even[:, 128:], odd[:, 128:])
             mix[these, lanes] = (top / low).astype(BF)
 
-    attend_row(0)
-
     shared(xcls.at[core, own], xcls_place, xs_sem, xr_sem)
     xcls_over = remote(xcls.at[core], xcls.at[core], fs_sem.at[10], fr_sem.at[10], (enc, sibling))
     xcls_over.start()
     xcls_back = remote(xcls.at[core], xcls.at[1 - core], fs_sem.at[10], fr_sem.at[10], (enc, sibling))
     shared(mixed.at[own], mixed_place, ms_sem, mr_sem)
+    send_pieces(px, recv_v, range(n), vs_sem, vr_sem)
     loads[4].wait()
 
     acc[...] = nn(mixed[...], w_out[...]) + o_bias[...] + xcls[core].astype(F32)
@@ -748,15 +756,10 @@
         place = lax.rem(device, 2) * side + lax.div(device, 2) * PAD
         return place + question - device * local
 
-    place_row = iota((1, 2 * side), 1)
-
-    def place_step(device, row):
-        for k in range(local):
-            question = device * local + k
-            row = jnp.where(place_row == padded(question), padded(positives[question]), row)
-        return row
-
-    pos_row = lax.fori_loop(0, n, place_step, jnp.full((1, 2 * side), -1, jnp.int32))
+    count = n * local
+    spot = padded(iota((count, 1), 0)) == iota((count, 2 * side), 1)
+    goal = padded(positives[...].reshape(1, count)) + 1
+    pos_row = nn(goal.astype(F32).astype(BF), spot.astype(F32).astype(BF)).astype(jnp.int32) - 1
 
     xcls_back.wait_recv()
 
@@ -768,9 +771,6 @@
 
     save(xcls.at[0], xcls_o.at[pl.ds(0, side)], 4)
     save(xcls.at[1], xcls_o.at[pl.ds(side, side)], 5)
-
-    attend_row(1)
-    attend_row(2)
 
     cls_copy(enc, core, 0, (other, me)).wait_send()
     cls_in = remote(cls.at[enc, core], cls.at[other, core], cs_sem.at[0], cr_sem.at[0], (other, me))
@@ -842,9 +842,7 @@
     dmix_over = remote(dmix.at[core], dmix.at[core], fs_sem.at[11], fr_sem.at[11], (enc, sibling))
     dmix_back = remote(dmix.at[core], dmix.at[1 - core], fs_sem.at[11], fr_sem.at[11], (enc, sibling))
 
-    @pl.when(core == 0)
-    def _():
-        dmix_over.start()
+    dmix_over.start()
 
     block_diagonal(dbd, dmix[core, own, :].astype(F32))
     d_weights = nt(dbd[...], kv[:, pl.ds(width, width)])
@@ -852,14 +850,12 @@
     inner_sum = jnp.sum(d_weights * weights, -1, keepdims=True)
     ds_low[...] = (head_scale * weights * (d_weights - inner_sum)).astype(BF)
     dx[...] = nn(ds_low[...], x[...]).astype(BF)
-    send_pieces(dx, 0, ks_sem)
+    send_pieces(dx, recv, key_owners, ks_sem, kr_sem)
     dq_own[...] = own_lanes(nn(ds_low[...], kv[:, pl.ds(0, width)])).astype(BF)
 
     def dq_place(peer):
         return dq_o.at[block(slot_of(peer))]
 
-    queries = Relay(dq_own, dq_place, qs_sem, qr_sem)
-    queries.start()
     save(dq_own, dq_place(me), 6)
     give(douter, douter_o, 7)
     give(dinner, dinner_o, 8)
@@ -879,51 +875,62 @@
         hout[these, :] = (unit * gain2[...] + shift2[...]).astype(BF)
         save(hout.at[these], hidden_out.at[these], 13 + r)
 
-    group = lax.rem(which, 4)
-
-    def grad_place(peer):
-        index = lax.div(peer, 2)
+    def piece_place(matrix, i):
         return kv_o.at[
-            lax.rem(peer, 2),
-            pl.ds(pl.multiple_of(lax.rem(index, 4) * group_cols, group_cols), group_cols),
-            pl.ds(pl.multiple_of(lax.div(index, 4) * half_feats, half_feats), half_feats),
+            matrix,
+            pl.ds(pl.multiple_of(lax.rem(i, 4) * group_cols, group_cols), group_cols),
+            pl.ds(pl.multiple_of(lax.div(i, 4) * half_feats, half_feats), half_feats),
         ]
 
-    summed = Relay(piece, grad_place, gs_sem, gr_sem)
-    piece_save = pltpu.make_async_copy(piece, grad_place(me), save_sem.at[16])
-
-    def sum_pieces():
-        def came(j):
-            peer = lax.rem(me + j + 1, n)
-            place = recv.at[slot_of(peer)]
-            remote(place, place, ks_sem.at[0], kr_sem.at[peer], (enc, peer)).wait_recv()
-
-        loop(n - 1, came)
+    def key_place(peer):
+        return piece_place(0, lax.div(peer, 2))
+
+    def value_place(peer):
+        return piece_place(1, lax.rem(peer, half_n))
+
+    keys = Relay(piece, key_place, gs_sem, gr_sem, n)
+    values = Relay(piece_v, value_place, hs_sem, hr_sem, half_n)
+    key_save = pltpu.make_async_copy(piece, key_place(me), save_sem.at[16])
+
+    def sum_pieces(i, left, right, target):
         for a in range(H // 4):
-            right = recv[:, pl.ds(a * PAD, PAD), :].reshape(2 * side, half_feats)
-            left = turned[pl.ds(pl.multiple_of(group * group_cols + a * head, head), head), :]
-            piece[pl.ds(a * head, head), :] = nn(left, right).astype(BF)
-        summed.start()
-        piece_save.start()
-
-    @pl.when(core == 1)
-    def _():
-        dmix_back.wait_recv()
-        for c in range(2):
-            turned[:, pl.ds(c * side, side)] = dmix[c].astype(F32).T.astype(BF)
-        sum_pieces()
-
-    layer_tile(0)
-    layer_tile(1)
-    queries.plane()
+            rows_a = right[:, pl.ds(a * PAD, PAD), :].reshape(2 * side, half_feats)
+            start = lax.rem(i, 4) * group_cols + a * head
+            cols_a = left[pl.ds(pl.multiple_of(start, head), head), :]
+            target[pl.ds(a * head, head), :] = nn(cols_a, rows_a).astype(BF)
+
+    pieces_came(recv_v, vr_sem)
+    dmix_back.wait_recv()
+    for c in range(2):
+        turned_v[:, pl.ds(c * side, side)] = dmix[c].astype(F32).T.astype(BF)
+    sum_pieces(lax.rem(me, half_n), turned_v, recv_v, piece_v)
+    values.start()
+    save(piece_v, value_place(me), 10)
+
+    y = nn(x[...], w_qkv[:, query_w]) + q_bias[...]
+    q[...] = (y.astype(BF).astype(F32) * head_scale).astype(BF)
+    for r in range(rows):
+        attend_row(r)
+    values.plane()
 
     @pl.when(core == 0)
     def _():
-        sum_pieces()
+        pieces_came(recv, kr_sem)
+        sum_pieces(which, turned, recv, piece)
+        keys.start()
+        key_save.start()
+
+    layer_tile(0)
+    values.over()
+    layer_tile(1)
+    share(dq_own, dq_place, qs_sem, qr_sem)
+    remote(dq_own, dq_place(me), qs_sem.at[n - 2], qr_sem.at[me], (enc, sibling)).start()
+
+    @pl.when(core == 0)
+    def _():
+        keys.plane()
 
     layer_tile(2)
-    queries.over()
-    summed.plane()
 
     base = dfirst[own, :] + nt(dq_own[...], w_qkv[:, query_w])
     base = base.astype(BF)
@@ -937,23 +944,49 @@
     vecs_take = remote(vecs, vecs_o.at[1 - core], fs_sem.at[12], fr_sem.at[12], (enc, sibling))
     save(vecs, vecs_o.at[core], 12)
 
-    summed.over()
-    sent_pieces(px, 1, vs_sem)
-    sent_pieces(dx, 0, ks_sem)
-    queries.sent()
-    queries.came()
-    xcls_back.wait_send()
+    def dq_pass(j):
+        peer = same_core(j)
+        remote(dq_own, dq_place(peer), qs_sem.at[j], qr_sem.at[peer], (enc, peer)).wait_recv()
+        send = qs_sem.at[n // 2 - 1 + j]
+        remote(dq_place(peer), dq_place(peer), send, qr_sem.at[peer], (enc, sibling)).start()
+
+    loop(n // 2 - 1, dq_pass)
 
     @pl.when(core == 0)
     def _():
-        dmix_over.wait_send()
-
+        keys.over()
+
+    sent_pieces(px, recv_v, range(n), vs_sem, vr_sem)
+    sent_pieces(dx, recv, key_owners, ks_sem, kr_sem)
+
+    def dq_came(j):
+        peer = cousin(j)
+        remote(dq_own, dq_place(peer), qs_sem.at[0], qr_sem.at[peer], (enc, sibling)).wait_recv()
+
+    loop(n // 2, dq_came)
+
+    def dq_sent(j):
+        remote(dq_own, dq_place(me), qs_sem.at[j], qr_sem.at[me], (enc, sibling)).wait_send()
+
+    loop(n - 1, dq_sent)
+    xcls_back.wait_send()
+
+    dmix_over.wait_send()
     for copy in [*given, vecs_take]:
         copy.wait_send()
         copy.wait_recv()
-    summed.sent()
-    piece_save.wait()
-    summed.came()
+    values.sent()
+    values.came()
+
+    @pl.when(core == 0)
+    def _():
+        keys.sent()
+        key_save.wait()
+
+    @pl.when(core == 1)
+    def _():
+        keys.came()
+
     for copy in saves:
         copy.wait()
 
@@ -1132,7 +1165,7 @@
             shape((2, 8, width), F32),
             shape((2, width, width), BF),
         ],
-        in_specs=[smem, smem, hbm, hbm, vmem, vmem, hbm, vmem, vmem, vmem, hbm, vmem, hbm, vmem, vmem, vmem],
+        in_specs=[smem, vmem, hbm, hbm, vmem, vmem, hbm, vmem, vmem, vmem, hbm, vmem, hbm, vmem, vmem, vmem],
         out_specs=[hbm] * 12,
         scratch_shapes=[
             pltpu.VMEM((tokens, width), BF),
@@ -1174,6 +1207,9 @@
             pltpu.VMEM((width, wide), BF),
             pltpu.VMEM((n, H // 4 * PAD, width // 2), BF),
             pltpu.VMEM((width // 4, width // 2), BF),
+            pltpu.VMEM((width, wide), BF),
+            pltpu.VMEM((n, H // 4 * PAD, width // 2), BF),
+            pltpu.VMEM((width // 4, width // 2), BF),
             pltpu.VMEM((PAD, width), BF),
             pltpu.VMEM((length, width), BF),
             pltpu.VMEM((length, width), F32),
@@ -1189,10 +1225,13 @@
             dma((n,)),
             dma((3,)),
             dma((3,)),
-            dma((4 * planes,)),
+            dma((n - 1,)),
             dma((n,)),
-            dma((n // 2,)),
-            dma((4 * planes,)),
+            dma((n,)),
+            dma((n,)),
+            dma((n,)),
+            dma((n,)),
+            dma((n,)),
             dma((n,)),
             dma((13,)),
             dma((13,)),
@@ -1202,7 +1241,7 @@
         ),
         name="layer",
     )(
-        starts,
+        jnp.transpose(starts, (1, 0, 2)),
         positives,
         hidden_in.reshape(tokens, width),
         qkv_weight.reshape(width, 3 * width),

time: 86.3 us -> 80 us (0.927)
  the two profiles are of different devices: /device:TPU:25 before, /device:TPU:0 now
where the time goes in v4:
time: 80 us; the launch traced here: 79.8 us
  Pallas kernels  78.9 us (99%)
  between operations  0.84 us (1%)
    pallas_call x1, Pallas kernels, fused_on_device(): pl.pallas_call(functools.partial(main_kernel, n), out_shape=[shape((token...  64.7 us
    pallas_call x1, Pallas kernels, fused_on_device(): pl.pallas_call(grad_kernel, out_shape=[shape((1, 1), F32), shape((tokens,...  14.2 us

profile of v4, /device:TPU:0, one launch (start us, length us, event | category | flops | bytes accessed | tf_op | source)
XLA Modules:
  0.0 79.8 jit_solution(3662099389247039348)
XLA Ops:
  0.7 64.7 %layer.1 = (bf16[768,768]{1,0:T(8,128)(2,1)}, bf16[768,768]{1,0:T(8,128)(2,1)}, bf16[256,768]{1,0:T(8,128)(2,1)}, bf16[256,768]{1,0:T(8,128)(2,1)}, bf16[256,768...) custom-call(s32[3,1,4]{2,1,0:T(1,128)} %bitcast.14, ...), custom_call_target="tpu_custom_call" | custom-call | tf_op jit(solution)/shard_map/layer/pallas_call | solution.py:1152
  65.4 14.2 %gradients.1 = (f32[1,1]{1,0:T(1,128)}, bf16[768,768]{1,0:T(8,128)(2,1)}, bf16[768,768]{1,0:T(8,128)(2,1)}, f32[1,768,2304]{2,1,0:T(8,128)}, f32[1,768]{1,0:T(1,...) custom-call(bf16[256,768]{1,0:T(8,128)(2,1)} %get-tuple-element.44.x, ...), custom_call_target="tpu_custom_call" | custom-call | tf_op jit(solution)/shard_map/gradients/pallas_call | solution.py:1263

commit v5 on v4

--- a/solution.py
+++ b/solution.py
@@ -356,6 +356,10 @@
     w_out,
     w_up,
     w_down,
+    out_turned,
+    up_turned,
+    down_turned,
+    v_turned,
     kv,
     q,
     mix,
@@ -679,6 +683,11 @@
 
     key_owners = range(0, n, 2)
     px[...] = nn(p_low[...], x[...]).astype(BF)
+    v_turned[...] = kv[:, pl.ds(width, width)].T
+    y = nn(x[...], w_qkv[:, query_w]) + q_bias[...]
+    q[...] = (y.astype(BF).astype(F32) * head_scale).astype(BF)
+    loads[5].wait()
+    up_turned[...] = w_up[...].T
     def attend_row(r):
         place0 = iota((length, 1), 0)
         place1 = iota((1, length), 1)
@@ -709,6 +718,8 @@
             low = jnp.where(low_half, even[:, 128:], odd[:, 128:])
             mix[these, lanes] = (top / low).astype(BF)
 
+    attend_row(0)
+
     shared(xcls.at[core, own], xcls_place, xs_sem, xr_sem)
     xcls_over = remote(xcls.at[core], xcls.at[core], fs_sem.at[10], fr_sem.at[10], (enc, sibling))
     xcls_over.start()
@@ -729,7 +740,6 @@
     inv1[...] = jnp.broadcast_to(inverse, inv1.shape)
     level = unit * gain1[...] + shift1[...]
     normed[...] = level.astype(BF)
-    loads[5].wait()
     loads[6].wait()
     inner = nn(normed[...], w_up[...]) + u_bias[...]
     cdf, pdf = gelu_parts(inner)
@@ -760,6 +770,10 @@
     spot = padded(iota((count, 1), 0)) == iota((count, 2 * side), 1)
     goal = padded(positives[...].reshape(1, count)) + 1
     pos_row = nn(goal.astype(F32).astype(BF), spot.astype(F32).astype(BF)).astype(jnp.int32) - 1
+
+    down_turned[...] = w_down[...].T
+    out_turned[...] = w_out[...].T
+    attend_row(1)
 
     xcls_back.wait_recv()
 
@@ -827,9 +841,9 @@
     vecs[pl.ds(1, 1), :] = column_sum(d_cls[...])
     d_second = back(d_cls[...], norm2[...], inv2[...], gain2[...])
     douter[...] = d_second.astype(BF)
-    d_active = nt(douter[...], w_down[...])
+    d_active = nn(douter[...], down_turned[...])
     dinner[...] = (d_active * slope[...]).astype(BF)
-    acc[...] = d_second + nt(dinner[...], w_up[...])
+    acc[...] = d_second + nn(dinner[...], up_turned[...])
     vecs[pl.ds(2, 1), :] = column_sum(acc[...] * norm1[...])
     vecs[pl.ds(3, 1), :] = column_sum(acc[...])
     vecs[pl.ds(4, 1), :] = jnp.broadcast_to(loss, (1, width))
@@ -838,14 +852,14 @@
     dfirst[...] = d_first
     datt[...] = d_first.astype(BF)
 
-    dmix[core] = nt(datt[...], w_out[...]).astype(BF)
+    dmix[core] = nn(datt[...], out_turned[...]).astype(BF)
     dmix_over = remote(dmix.at[core], dmix.at[core], fs_sem.at[11], fr_sem.at[11], (enc, sibling))
     dmix_back = remote(dmix.at[core], dmix.at[1 - core], fs_sem.at[11], fr_sem.at[11], (enc, sibling))
 
     dmix_over.start()
 
     block_diagonal(dbd, dmix[core, own, :].astype(F32))
-    d_weights = nt(dbd[...], kv[:, pl.ds(width, width)])
+    d_weights = nn(dbd[...], v_turned[...])
     weights = probs[...]
     inner_sum = jnp.sum(d_weights * weights, -1, keepdims=True)
     ds_low[...] = (head_scale * weights * (d_weights - inner_sum)).astype(BF)
@@ -857,9 +871,6 @@
         return dq_o.at[block(slot_of(peer))]
 
     save(dq_own, dq_place(me), 6)
-    give(douter, douter_o, 7)
-    give(dinner, dinner_o, 8)
-    give(datt, datt_o, 9)
     vecs[pl.ds(5, 1), :] = column_sum(dmix[core].astype(F32))
 
     def layer_tile(r):
@@ -907,11 +918,8 @@
     values.start()
     save(piece_v, value_place(me), 10)
 
-    y = nn(x[...], w_qkv[:, query_w]) + q_bias[...]
-    q[...] = (y.astype(BF).astype(F32) * head_scale).astype(BF)
-    for r in range(rows):
+    for r in range(2, rows):
         attend_row(r)
-    values.plane()
 
     @pl.when(core == 0)
     def _():
@@ -920,9 +928,13 @@
         keys.start()
         key_save.start()
 
+    give(douter, douter_o, 7)
+    give(dinner, dinner_o, 8)
+    give(datt, datt_o, 9)
+    values.plane()
     layer_tile(0)
+    layer_tile(1)
     values.over()
-    layer_tile(1)
     share(dq_own, dq_place, qs_sem, qr_sem)
     remote(dq_own, dq_place(me), qs_sem.at[n - 2], qr_sem.at[me], (enc, sibling)).start()
 
@@ -951,44 +963,43 @@
         remote(dq_place(peer), dq_place(peer), send, qr_sem.at[peer], (enc, sibling)).start()
 
     loop(n // 2 - 1, dq_pass)
-
-    @pl.when(core == 0)
-    def _():
-        keys.over()
-
     sent_pieces(px, recv_v, range(n), vs_sem, vr_sem)
     sent_pieces(dx, recv, key_owners, ks_sem, kr_sem)
-
-    def dq_came(j):
-        peer = cousin(j)
-        remote(dq_own, dq_place(peer), qs_sem.at[0], qr_sem.at[peer], (enc, sibling)).wait_recv()
-
-    loop(n // 2, dq_came)
-
-    def dq_sent(j):
-        remote(dq_own, dq_place(me), qs_sem.at[j], qr_sem.at[me], (enc, sibling)).wait_send()
-
-    loop(n - 1, dq_sent)
     xcls_back.wait_send()
-
     dmix_over.wait_send()
     for copy in [*given, vecs_take]:
         copy.wait_send()
         copy.wait_recv()
     values.sent()
     values.came()
+    for copy in saves[:-1]:
+        copy.wait()
+
+    @pl.when(core == 0)
+    def _():
+        key_save.wait()
+        keys.over()
+
+    def dq_came(j):
+        peer = cousin(j)
+        remote(dq_own, dq_place(peer), qs_sem.at[0], qr_sem.at[peer], (enc, sibling)).wait_recv()
+
+    loop(n // 2, dq_came)
+
+    def dq_sent(j):
+        remote(dq_own, dq_place(me), qs_sem.at[j], qr_sem.at[me], (enc, sibling)).wait_send()
+
+    loop(n - 1, dq_sent)
 
     @pl.when(core == 0)
     def _():
         keys.sent()
-        key_save.wait()
 
     @pl.when(core == 1)
     def _():
         keys.came()
 
-    for copy in saves:
-        copy.wait()
+    saves[-1].wait()
 
 
 def grad_kernel(
@@ -1173,6 +1184,10 @@
             pltpu.VMEM((width, width), BF),
             pltpu.VMEM((width, ff), BF),
             pltpu.VMEM((ff, width), BF),
+            pltpu.VMEM((width, width), BF),
+            pltpu.VMEM((ff, width), BF),
+            pltpu.VMEM((width, ff), BF),
+            pltpu.VMEM((width, tokens), BF),
             pltpu.VMEM((tokens, 2 * width), BF),
             pltpu.VMEM((tokens, width), BF),
             pltpu.VMEM((tokens, width), BF),

time: 80 us -> 76.1 us (0.951)
  Pallas kernels: 78.9 us -> 75 us
    pallas_call x1, Pallas kernels: 64.7 us -> 60.7 us  [fused_on_device(): pl.pallas_call(functools.partial(main_kernel, n), out_shape=[shape((token...]
where the time goes in v5:
time: 76.1 us; the launch traced here: 75.8 us
  Pallas kernels  75 us (99%)
  between operations  0.84 us (1%)
    pallas_call x1, Pallas kernels, fused_on_device(): pl.pallas_call(functools.partial(main_kernel, n), out_shape=[shape((token...  60.7 us
    pallas_call x1, Pallas kernels, fused_on_device(): pl.pallas_call(grad_kernel, out_shape=[shape((1, 1), F32), shape((tokens,...  14.2 us

profile of v5, /device:TPU:0, one launch (start us, length us, event | category | flops | bytes accessed | tf_op | source)
XLA Modules:
  0.0 75.8 jit_solution(2404909058924578353)
XLA Ops:
  0.7 60.7 %layer.1 = (bf16[768,768]{1,0:T(8,128)(2,1)}, bf16[768,768]{1,0:T(8,128)(2,1)}, bf16[256,768]{1,0:T(8,128)(2,1)}, bf16[256,768]{1,0:T(8,128)(2,1)}, bf16[256,768...) custom-call(s32[3,1,4]{2,1,0:T(1,128)} %bitcast.14, ...), custom_call_target="tpu_custom_call" | custom-call | tf_op jit(solution)/shard_map/layer/pallas_call | solution.py:1163
  61.4 14.2 %gradients.1 = (f32[1,1]{1,0:T(1,128)}, bf16[768,768]{1,0:T(8,128)(2,1)}, bf16[768,768]{1,0:T(8,128)(2,1)}, f32[1,768,2304]{2,1,0:T(8,128)}, f32[1,768]{1,0:T(1,...) custom-call(bf16[256,768]{1,0:T(8,128)(2,1)} %get-tuple-element.44.x, ...), custom_call_target="tpu_custom_call" | custom-call | tf_op jit(solution)/shard_map/gradients/pallas_call | solution.py:1278

commit v6 on v5

--- a/solution.py
+++ b/solution.py
@@ -376,6 +376,7 @@
     xcls,
     mixed,
     cls,
+    packed,
     norm1,
     inv1,
     norm2,
@@ -750,9 +751,19 @@
     inv2[...] = jnp.broadcast_to(inverse, inv2.shape)
     cls[enc, core] = (unit * gain2[...] + shift2[...]).astype(BF)
 
+    dense = packed.shape[2]
+    order = iota((dense, 1), 0)
+    keep = iota((dense, side), 1) == order + (PAD - local) * lax.div(order, local)
+    keep = keep.astype(F32).astype(BF)
+    packed[enc, core] = nn(keep, cls[enc, core]).astype(BF)
+
+    def unpack(half_of, from_core):
+        cls[half_of, from_core] = tn(keep, packed[half_of, from_core]).astype(BF)
+
+
     def cls_copy(half_of, to_core, index, device):
         return remote(
-            cls.at[half_of, core], cls.at[half_of, to_core], cs_sem.at[index], cr_sem.at[index], device
+            packed.at[half_of, core], packed.at[half_of, to_core], cs_sem.at[index], cr_sem.at[index], device
         )
 
     cls_copy(enc, core, 0, (other, me)).start()
@@ -787,18 +798,23 @@
     save(xcls.at[1], xcls_o.at[pl.ds(side, side)], 5)
 
     cls_copy(enc, core, 0, (other, me)).wait_send()
-    cls_in = remote(cls.at[enc, core], cls.at[other, core], cs_sem.at[0], cr_sem.at[0], (other, me))
+    cls_in = remote(
+        packed.at[enc, core], packed.at[other, core], cs_sem.at[0], cr_sem.at[0], (other, me)
+    )
     cls_in.wait_recv()
     cls_pass = cls_copy(other, core, 2, (enc, sibling))
     cls_pass.start()
     cls_copy(enc, core, 1, (enc, sibling)).wait_send()
     remote(
-        cls.at[enc, core], cls.at[enc, 1 - core], cs_sem.at[1], cr_sem.at[1], (enc, sibling)
+        packed.at[enc, core], packed.at[enc, 1 - core], cs_sem.at[1], cr_sem.at[1], (enc, sibling)
     ).wait_recv()
+    unpack(enc, 1 - core)
+    unpack(other, core)
     cls_pass.wait_send()
     remote(
-        cls.at[other, core], cls.at[other, 1 - core], cs_sem.at[2], cr_sem.at[2], (enc, sibling)
+        packed.at[other, core], packed.at[other, 1 - core], cs_sem.at[2], cr_sem.at[2], (enc, sibling)
     ).wait_recv()
+    unpack(other, 1 - core)
 
     sim_scale = width ** (-0.5)
     good_col = lax.rem(iota((2 * side, 1), 0), PAD) < local
@@ -1204,6 +1220,7 @@
             pltpu.VMEM((2, side, width), BF),
             pltpu.VMEM((side, width), BF),
             pltpu.VMEM((2, 2, side, width), BF),
+            pltpu.VMEM((2, 2, side // PAD * rows * DOCS, width), BF),
             pltpu.VMEM((side, width), F32),
             pltpu.VMEM((side, 128), F32),
             pltpu.VMEM((side, width), F32),

time: 76.1 us -> 75.6 us (level)
  no operation moved by 1% of the time
where the time goes in v6:
time: 75.6 us; the launch traced here: 75.3 us
  Pallas kernels  74.5 us (99%)
  between operations  0.86 us (1%)
    pallas_call x1, Pallas kernels, fused_on_device(): pl.pallas_call(functools.partial(main_kernel, n), out_shape=[shape((token...  60.2 us
    pallas_call x1, Pallas kernels, fused_on_device(): pl.pallas_call(grad_kernel, out_shape=[shape((1, 1), F32), shape((tokens,...  14.2 us

profile of v6, /device:TPU:0, one launch (start us, length us, event | category | flops | bytes accessed | tf_op | source)
XLA Modules:
  0.0 75.3 jit_solution(7486150632300038332)
XLA Ops:
  0.7 60.2 %layer.1 = (bf16[768,768]{1,0:T(8,128)(2,1)}, bf16[768,768]{1,0:T(8,128)(2,1)}, bf16[256,768]{1,0:T(8,128)(2,1)}, bf16[256,768]{1,0:T(8,128)(2,1)}, bf16[256,768...) custom-call(s32[3,1,4]{2,1,0:T(1,128)} %bitcast.14, ...), custom_call_target="tpu_custom_call" | custom-call | tf_op jit(solution)/shard_map/layer/pallas_call | solution.py:1179
  60.9 14.2 %gradients.1 = (f32[1,1]{1,0:T(1,128)}, bf16[768,768]{1,0:T(8,128)(2,1)}, bf16[768,768]{1,0:T(8,128)(2,1)}, f32[1,768,2304]{2,1,0:T(8,128)}, f32[1,768]{1,0:T(1,...) custom-call(bf16[256,768]{1,0:T(8,128)(2,1)} %get-tuple-element.44.x, ...), custom_call_target="tpu_custom_call" | custom-call | tf_op jit(solution)/shard_map/gradients/pallas_call | solution.py:1295
